TPU v7x, 128 devices: a whole 4x4x4 slice. The times are simulated.
128 devices in a mesh: states: 64 (over z, y, x), act: 2 (over core).
Axes of the slice: x: 4, y: 4, z: 4, core: 2. Of those that a mesh axis runs over, the one named last changes fastest.
Arguments:
- transitions: float32 [4, 1024, 2, 128, 128], P('act', 'states'), may hold values from 7.8125e-05 to 0.01953125
- columns: int32 [4, 1024, 2], P(None, 'states'), may hold values from 0 to 1023, as said below
- targets: int32 [131072, 128], P('states'), may hold values 0 or 1
Outputs:
- values: float32 [131072, 128], P('states')
Inputs may be any that keep to these rules, and one draw needn't show every extreme that they name: columns[a, b, t] = (b + d) mod 1024 with |d| <= 8; both d = 8 and d = -8 occur in every draw.
All inputs are finite; a program needn't handle non-finite values. No bound on the sum of `targets` on one device may be relied on, other than what follows from the above.
Results may differ from a plain program's by a relative error of at most 0.0003.
Values sent between devices are 32-bit elements; how exact they have to be, the bound alone decides.
A program may use at most 64 MiB of HBM per device.

v0:
```python
import jax
import jax.numpy as jnp
from jax import lax
from jax.sharding import PartitionSpec as P

REACH = 8
SWEEPS = 12


def extended(cells, sides, width):
    for axis, dim in sides:
        count = lax.axis_size(axis)
        head = lax.slice_in_dim(cells, 0, width, axis=dim)
        tail = lax.slice_in_dim(cells, cells.shape[dim] - width, cells.shape[dim], axis=dim)
        cells = jnp.concatenate(
            [
                lax.ppermute(tail, axis, [(i, (i + 1) % count) for i in range(count)]),
                cells,
                lax.ppermute(head, axis, [((i + 1) % count, i) for i in range(count)]),
            ],
            axis=dim,
        )
    return cells


def extend(panel, width_rows):
    return extended(panel, (("states", 0),), width_rows)


def products(padded, tiles, column_ids, first_block, total_blocks, tile_rows, target_sets):
    blocks = padded.reshape(-1, tile_rows, target_sets)
    local_index = (column_ids - first_block + REACH) % total_blocks
    picked = blocks[local_index]
    values = jnp.einsum("arbij,arbjk->arik", tiles, picked, precision=lax.Precision.HIGHEST)
    return jnp.max(values, axis=0)


def per_device(transitions, columns, targets):
    acts_here = transitions.shape[0]
    row_blocks = transitions.shape[1]
    tile_rows = transitions.shape[3]
    target_sets = targets.shape[1]
    total_blocks = row_blocks * lax.axis_size("states")
    first_block = lax.axis_index("states") * row_blocks
    width_rows = REACH * tile_rows
    target_hit = targets == 1
    panel = targets.astype(jnp.float32)
    own_columns = lax.dynamic_slice_in_dim(columns, lax.axis_index("act") * acts_here, acts_here, 0)

    def action_sweep(sweep_index, current):
        padded = extend(current, width_rows)
        largest = products(
            padded, transitions, own_columns, first_block, total_blocks, tile_rows, target_sets
        )
        merged = lax.pmax(largest, "act")
        return jnp.where(target_hit, jnp.float32(1.0), merged.reshape(-1, target_sets))

    panel = lax.fori_loop(0, SWEEPS, action_sweep, panel)
    return panel


def solution(mesh):
    return jax.shard_map(
        per_device,
        mesh=mesh,
        in_specs=(P("act", "states", None, None, None), P(None, "states", None), P("states", None)),
        out_specs=P("states", None),
        check_vma=False,
    )
```

profile of v0, /device:TPU:0, one launch (start us, length us, event | category | flops | bytes accessed | tf_op | source)
XLA Modules:
  0.0 781.8 jit_solution(1219909621656360389)
XLA Ops:
  9.9 764.1 %while.12 = (s32[]{:T(128)}, f32[2048,128]{1,0:T(8,128)S(1)}, s32[]{:T(128)}, s32[2,16,2]{1,2,0:T(2,128)S(1)}, f32[2,16,2,128,128]{4,3,2,1,0:T(8,128)}, /*index=5*/pred[2048,128]{1,0:T(8,128)(4,1)S(1)}, s32[]{:T(128)}) while((s32[]{:T(128)}, f32[2048,128]{1,0:T(8,128)S(1)}, s32[]{:T(128)}, s32[2,16,2]{1,2,0:T(2,128)S(1)}, ...), condition=%wide.region_3.4_spmd, body=%wide.region_0.3_spmd.sunk | while | flops 1612449792 | bytes 41162980 | solution.py:58
  10.0 8.8 %collective-permute-start = (f32[1024,128]{1,0:T(8,128)S(1)}, f32[1024,128]{1,0:T(8,128)S(1)}, u32[]{:S(2)}, u32[]{:S(2)}) collective-permute-start(f32[1024,128]{1,0:T(8,128)S(1)} %get-tuple-element.137), channel_id=1, source_target_pairs={{2,0},{4,2},{6,4},{8,6},{10,8},{12,10},{14,12},{16,14},{18,16},{20... | collective-permute-start | bytes 1572872 | tf_op jit(solution)/shard_map/while/body/eval_jaxpr/ppermute | solution.py:19
  19.1 11.0 %collective-permute-done = f32[1024,128]{1,0:T(8,128)S(1)} collective-permute-done((f32[1024,128]{1,0:T(8,128)S(1)}, f32[1024,128]{1,0:T(8,128)S(1)}, u32[]{:S(2)}, u32[]{:S(2)}) %collective-permute-start) | collective-permute-done | bytes 524320 | tf_op jit(solution)/shard_map/while/body/eval_jaxpr/ppermute | solution.py:19
  41.9 10.3 %bitcast_reduce_fusion.2 = f32[16,128,128]{2,1,0:T(8,128)S(1)} fusion(f32[2,16,2,128,128]{4,3,2,1,0:T(8,128)} %bitcast.33, f32[2,16,2,128,128]{4,3,2,1,0:T(8,128)} %get-tuple-element.157), kind=kOutput, calls=%fused_computation.2.clone.1 | convolution fusion | flops 1610874880 | bytes 9437184 | tf_op jit(solution)/shard_map/while/body/eval_jaxpr/arbij,arbjk->arik/dot_general | solution.py:34
  53.6 19.5 %all-reduce.2.cloned.1.call-done = f32[2048,128]{1,0:T(8,128)} async-done(((f32[2048,128]{1,0:T(8,128)}), f32[2048,128]{1,0:T(8,128)}) %all-reduce.2.cloned.1.call-update) | async-done | bytes 1048592 | tf_op jit(solution)/shard_map/while/body/eval_jaxpr/pmax | solution.py:55
  74.6 7.4 collective-permute-start
  82.2 11.4 %collective-permute-done = f32[1024,128]{1,0:T(8,128)S(1)} collective-permute-done((f32[1024,128]{1,0:T(8,128)S(1)}, f32[1024,128]{1,0:T(8,128)S(1)}, u32[]{:S(2)}, u32[]{:S(2)}) %collective-permute-start) | collective-permute-done | bytes 524320 | tf_op jit(solution)/shard_map/while/body/eval_jaxpr/ppermute | solution.py:19
  105.5 10.3 %bitcast_reduce_fusion.2 = f32[16,128,128]{2,1,0:T(8,128)S(1)} fusion(f32[2,16,2,128,128]{4,3,2,1,0:T(8,128)} %bitcast.33, f32[2,16,2,128,128]{4,3,2,1,0:T(8,128)} %get-tuple-element.157), kind=kOutput, calls=%fused_computation.2.clone.1 | convolution fusion | flops 1610874880 | bytes 9437184 | tf_op jit(solution)/shard_map/while/body/eval_jaxpr/arbij,arbjk->arik/dot_general | solution.py:34
  117.2 19.5 %all-reduce.2.cloned.1.call-done = f32[2048,128]{1,0:T(8,128)} async-done(((f32[2048,128]{1,0:T(8,128)}), f32[2048,128]{1,0:T(8,128)}) %all-reduce.2.cloned.1.call-update) | async-done | bytes 1048592 | tf_op jit(solution)/shard_map/while/body/eval_jaxpr/pmax | solution.py:55
  138.2 7.4 collective-permute-start
  145.8 11.4 %collective-permute-done = f32[1024,128]{1,0:T(8,128)S(1)} collective-permute-done((f32[1024,128]{1,0:T(8,128)S(1)}, f32[1024,128]{1,0:T(8,128)S(1)}, u32[]{:S(2)}, u32[]{:S(2)}) %collective-permute-start) | collective-permute-done | bytes 524320 | tf_op jit(solution)/shard_map/while/body/eval_jaxpr/ppermute | solution.py:19
  169.1 10.3 %bitcast_reduce_fusion.2 = f32[16,128,128]{2,1,0:T(8,128)S(1)} fusion(f32[2,16,2,128,128]{4,3,2,1,0:T(8,128)} %bitcast.33, f32[2,16,2,128,128]{4,3,2,1,0:T(8,128)} %get-tuple-element.157), kind=kOutput, calls=%fused_computation.2.clone.1 | convolution fusion | flops 1610874880 | bytes 9437184 | tf_op jit(solution)/shard_map/while/body/eval_jaxpr/arbij,arbjk->arik/dot_general | solution.py:34
  180.7 19.5 %all-reduce.2.cloned.1.call-done = f32[2048,128]{1,0:T(8,128)} async-done(((f32[2048,128]{1,0:T(8,128)}), f32[2048,128]{1,0:T(8,128)}) %all-reduce.2.cloned.1.call-update) | async-done | bytes 1048592 | tf_op jit(solution)/shard_map/while/body/eval_jaxpr/pmax | solution.py:55
  201.8 7.4 collective-permute-start
  209.4 11.4 %collective-permute-done = f32[1024,128]{1,0:T(8,128)S(1)} collective-permute-done((f32[1024,128]{1,0:T(8,128)S(1)}, f32[1024,128]{1,0:T(8,128)S(1)}, u32[]{:S(2)}, u32[]{:S(2)}) %collective-permute-start) | collective-permute-done | bytes 524320 | tf_op jit(solution)/shard_map/while/body/eval_jaxpr/ppermute | solution.py:19
  232.7 10.3 %bitcast_reduce_fusion.2 = f32[16,128,128]{2,1,0:T(8,128)S(1)} fusion(f32[2,16,2,128,128]{4,3,2,1,0:T(8,128)} %bitcast.33, f32[2,16,2,128,128]{4,3,2,1,0:T(8,128)} %get-tuple-element.157), kind=kOutput, calls=%fused_computation.2.clone.1 | convolution fusion | flops 1610874880 | bytes 9437184 | tf_op jit(solution)/shard_map/while/body/eval_jaxpr/arbij,arbjk->arik/dot_general | solution.py:34
  244.3 19.5 %all-reduce.2.cloned.1.call-done = f32[2048,128]{1,0:T(8,128)} async-done(((f32[2048,128]{1,0:T(8,128)}), f32[2048,128]{1,0:T(8,128)}) %all-reduce.2.cloned.1.call-update) | async-done | bytes 1048592 | tf_op jit(solution)/shard_map/while/body/eval_jaxpr/pmax | solution.py:55
  265.4 7.4 collective-permute-start
  273.0 11.4 %collective-permute-done = f32[1024,128]{1,0:T(8,128)S(1)} collective-permute-done((f32[1024,128]{1,0:T(8,128)S(1)}, f32[1024,128]{1,0:T(8,128)S(1)}, u32[]{:S(2)}, u32[]{:S(2)}) %collective-permute-start) | collective-permute-done | bytes 524320 | tf_op jit(solution)/shard_map/while/body/eval_jaxpr/ppermute | solution.py:19
  296.2 10.3 %bitcast_reduce_fusion.2 = f32[16,128,128]{2,1,0:T(8,128)S(1)} fusion(f32[2,16,2,128,128]{4,3,2,1,0:T(8,128)} %bitcast.33, f32[2,16,2,128,128]{4,3,2,1,0:T(8,128)} %get-tuple-element.157), kind=kOutput, calls=%fused_computation.2.clone.1 | convolution fusion | flops 1610874880 | bytes 9437184 | tf_op jit(solution)/shard_map/while/body/eval_jaxpr/arbij,arbjk->arik/dot_general | solution.py:34
  307.9 19.6 %all-reduce.2.cloned.1.call-done = f32[2048,128]{1,0:T(8,128)} async-done(((f32[2048,128]{1,0:T(8,128)}), f32[2048,128]{1,0:T(8,128)}) %all-reduce.2.cloned.1.call-update) | async-done | bytes 1048592 | tf_op jit(solution)/shard_map/while/body/eval_jaxpr/pmax | solution.py:55
  329.0 7.4 collective-permute-start
  336.6 11.4 %collective-permute-done = f32[1024,128]{1,0:T(8,128)S(1)} collective-permute-done((f32[1024,128]{1,0:T(8,128)S(1)}, f32[1024,128]{1,0:T(8,128)S(1)}, u32[]{:S(2)}, u32[]{:S(2)}) %collective-permute-start) | collective-permute-done | bytes 524320 | tf_op jit(solution)/shard_map/while/body/eval_jaxpr/ppermute | solution.py:19
  359.8 10.3 %bitcast_reduce_fusion.2 = f32[16,128,128]{2,1,0:T(8,128)S(1)} fusion(f32[2,16,2,128,128]{4,3,2,1,0:T(8,128)} %bitcast.33, f32[2,16,2,128,128]{4,3,2,1,0:T(8,128)} %get-tuple-element.157), kind=kOutput, calls=%fused_computation.2.clone.1 | convolution fusion | flops 1610874880 | bytes 9437184 | tf_op jit(solution)/shard_map/while/body/eval_jaxpr/arbij,arbjk->arik/dot_general | solution.py:34
  371.5 19.5 %all-reduce.2.cloned.1.call-done = f32[2048,128]{1,0:T(8,128)} async-done(((f32[2048,128]{1,0:T(8,128)}), f32[2048,128]{1,0:T(8,128)}) %all-reduce.2.cloned.1.call-update) | async-done | bytes 1048592 | tf_op jit(solution)/shard_map/while/body/eval_jaxpr/pmax | solution.py:55
  392.6 7.4 collective-permute-start
  400.2 11.4 %collective-permute-done = f32[1024,128]{1,0:T(8,128)S(1)} collective-permute-done((f32[1024,128]{1,0:T(8,128)S(1)}, f32[1024,128]{1,0:T(8,128)S(1)}, u32[]{:S(2)}, u32[]{:S(2)}) %collective-permute-start) | collective-permute-done | bytes 524320 | tf_op jit(solution)/shard_map/while/body/eval_jaxpr/ppermute | solution.py:19
  423.4 10.3 %bitcast_reduce_fusion.2 = f32[16,128,128]{2,1,0:T(8,128)S(1)} fusion(f32[2,16,2,128,128]{4,3,2,1,0:T(8,128)} %bitcast.33, f32[2,16,2,128,128]{4,3,2,1,0:T(8,128)} %get-tuple-element.157), kind=kOutput, calls=%fused_computation.2.clone.1 | convolution fusion | flops 1610874880 | bytes 9437184 | tf_op jit(solution)/shard_map/while/body/eval_jaxpr/arbij,arbjk->arik/dot_general | solution.py:34
  435.1 19.5 %all-reduce.2.cloned.1.call-done = f32[2048,128]{1,0:T(8,128)} async-done(((f32[2048,128]{1,0:T(8,128)}), f32[2048,128]{1,0:T(8,128)}) %all-reduce.2.cloned.1.call-update) | async-done | bytes 1048592 | tf_op jit(solution)/shard_map/while/body/eval_jaxpr/pmax | solution.py:55
  456.1 7.4 collective-permute-start
  463.8 11.4 %collective-permute-done = f32[1024,128]{1,0:T(8,128)S(1)} collective-permute-done((f32[1024,128]{1,0:T(8,128)S(1)}, f32[1024,128]{1,0:T(8,128)S(1)}, u32[]{:S(2)}, u32[]{:S(2)}) %collective-permute-start) | collective-permute-done | bytes 524320 | tf_op jit(solution)/shard_map/while/body/eval_jaxpr/ppermute | solution.py:19
  487.0 10.3 %bitcast_reduce_fusion.2 = f32[16,128,128]{2,1,0:T(8,128)S(1)} fusion(f32[2,16,2,128,128]{4,3,2,1,0:T(8,128)} %bitcast.33, f32[2,16,2,128,128]{4,3,2,1,0:T(8,128)} %get-tuple-element.157), kind=kOutput, calls=%fused_computation.2.clone.1 | convolution fusion | flops 1610874880 | bytes 9437184 | tf_op jit(solution)/shard_map/while/body/eval_jaxpr/arbij,arbjk->arik/dot_general | solution.py:34
  498.7 19.5 %all-reduce.2.cloned.1.call-done = f32[2048,128]{1,0:T(8,128)} async-done(((f32[2048,128]{1,0:T(8,128)}), f32[2048,128]{1,0:T(8,128)}) %all-reduce.2.cloned.1.call-update) | async-done | bytes 1048592 | tf_op jit(solution)/shard_map/while/body/eval_jaxpr/pmax | solution.py:55
  519.7 7.4 collective-permute-start
  527.4 11.4 %collective-permute-done = f32[1024,128]{1,0:T(8,128)S(1)} collective-permute-done((f32[1024,128]{1,0:T(8,128)S(1)}, f32[1024,128]{1,0:T(8,128)S(1)}, u32[]{:S(2)}, u32[]{:S(2)}) %collective-permute-start) | collective-permute-done | bytes 524320 | tf_op jit(solution)/shard_map/while/body/eval_jaxpr/ppermute | solution.py:19
  550.6 10.3 %bitcast_reduce_fusion.2 = f32[16,128,128]{2,1,0:T(8,128)S(1)} fusion(f32[2,16,2,128,128]{4,3,2,1,0:T(8,128)} %bitcast.33, f32[2,16,2,128,128]{4,3,2,1,0:T(8,128)} %get-tuple-element.157), kind=kOutput, calls=%fused_computation.2.clone.1 | convolution fusion | flops 1610874880 | bytes 9437184 | tf_op jit(solution)/shard_map/while/body/eval_jaxpr/arbij,arbjk->arik/dot_general | solution.py:34
  562.3 19.5 %all-reduce.2.cloned.1.call-done = f32[2048,128]{1,0:T(8,128)} async-done(((f32[2048,128]{1,0:T(8,128)}), f32[2048,128]{1,0:T(8,128)}) %all-reduce.2.cloned.1.call-update) | async-done | bytes 1048592 | tf_op jit(solution)/shard_map/while/body/eval_jaxpr/pmax | solution.py:55
  583.3 7.4 collective-permute-start
  591.0 11.4 %collective-permute-done = f32[1024,128]{1,0:T(8,128)S(1)} collective-permute-done((f32[1024,128]{1,0:T(8,128)S(1)}, f32[1024,128]{1,0:T(8,128)S(1)}, u32[]{:S(2)}, u32[]{:S(2)}) %collective-permute-start) | collective-permute-done | bytes 524320 | tf_op jit(solution)/shard_map/while/body/eval_jaxpr/ppermute | solution.py:19
  614.2 10.3 %bitcast_reduce_fusion.2 = f32[16,128,128]{2,1,0:T(8,128)S(1)} fusion(f32[2,16,2,128,128]{4,3,2,1,0:T(8,128)} %bitcast.33, f32[2,16,2,128,128]{4,3,2,1,0:T(8,128)} %get-tuple-element.157), kind=kOutput, calls=%fused_computation.2.clone.1 | convolution fusion | flops 1610874880 | bytes 9437184 | tf_op jit(solution)/shard_map/while/body/eval_jaxpr/arbij,arbjk->arik/dot_general | solution.py:34
  625.9 19.5 %all-reduce.2.cloned.1.call-done = f32[2048,128]{1,0:T(8,128)} async-done(((f32[2048,128]{1,0:T(8,128)}), f32[2048,128]{1,0:T(8,128)}) %all-reduce.2.cloned.1.call-update) | async-done | bytes 1048592 | tf_op jit(solution)/shard_map/while/body/eval_jaxpr/pmax | solution.py:55
  646.9 7.4 collective-permute-start
  654.6 11.4 %collective-permute-done = f32[1024,128]{1,0:T(8,128)S(1)} collective-permute-done((f32[1024,128]{1,0:T(8,128)S(1)}, f32[1024,128]{1,0:T(8,128)S(1)}, u32[]{:S(2)}, u32[]{:S(2)}) %collective-permute-start) | collective-permute-done | bytes 524320 | tf_op jit(solution)/shard_map/while/body/eval_jaxpr/ppermute | solution.py:19
  677.8 10.3 %bitcast_reduce_fusion.2 = f32[16,128,128]{2,1,0:T(8,128)S(1)} fusion(f32[2,16,2,128,128]{4,3,2,1,0:T(8,128)} %bitcast.33, f32[2,16,2,128,128]{4,3,2,1,0:T(8,128)} %get-tuple-element.157), kind=kOutput, calls=%fused_computation.2.clone.1 | convolution fusion | flops 1610874880 | bytes 9437184 | tf_op jit(solution)/shard_map/while/body/eval_jaxpr/arbij,arbjk->arik/dot_general | solution.py:34
  689.5 19.5 %all-reduce.2.cloned.1.call-done = f32[2048,128]{1,0:T(8,128)} async-done(((f32[2048,128]{1,0:T(8,128)}), f32[2048,128]{1,0:T(8,128)}) %all-reduce.2.cloned.1.call-update) | async-done | bytes 1048592 | tf_op jit(solution)/shard_map/while/body/eval_jaxpr/pmax | solution.py:55
  718.2 11.4 %collective-permute-done = f32[1024,128]{1,0:T(8,128)S(1)} collective-permute-done((f32[1024,128]{1,0:T(8,128)S(1)}, f32[1024,128]{1,0:T(8,128)S(1)}, u32[]{:S(2)}, u32[]{:S(2)}) %collective-permute-start) | collective-permute-done | bytes 524320 | tf_op jit(solution)/shard_map/while/body/eval_jaxpr/ppermute | solution.py:19
  741.4 10.3 %bitcast_reduce_fusion.2 = f32[16,128,128]{2,1,0:T(8,128)S(1)} fusion(f32[2,16,2,128,128]{4,3,2,1,0:T(8,128)} %bitcast.33, f32[2,16,2,128,128]{4,3,2,1,0:T(8,128)} %get-tuple-element.157), kind=kOutput, calls=%fused_computation.2.clone.1 | convolution fusion | flops 1610874880 | bytes 9437184 | tf_op jit(solution)/shard_map/while/body/eval_jaxpr/arbij,arbjk->arik/dot_general | solution.py:34
  753.1 19.5 %all-reduce.2.cloned.1.call-done = f32[2048,128]{1,0:T(8,128)} async-done(((f32[2048,128]{1,0:T(8,128)}), f32[2048,128]{1,0:T(8,128)}) %all-reduce.2.cloned.1.call-update) | async-done | bytes 1048592 | tf_op jit(solution)/shard_map/while/body/eval_jaxpr/pmax | solution.py:55
  (188 shorter events, 189.4 us)
Async XLA Ops:
  9.9 63.2 %all-reduce.2.cloned.1.call-start = ((), (), s32[]{:S(2)}) async-start(), calls=%async_computation | async-start | bytes 2097152 | tf_op jit(solution)/shard_map/while/body/eval_jaxpr/pmax | solution.py:55
  10.0 20.0 %collective-permute-start = (f32[1024,128]{1,0:T(8,128)S(1)}, f32[1024,128]{1,0:T(8,128)S(1)}, u32[]{:S(2)}, u32[]{:S(2)}) collective-permute-start(f32[1024,128]{1,0:T(8,128)S(1)} %get-tuple-element.137), channel_id=1, source_target_pairs={{2,0},{4,2},{6,4},{8,6},{10,8},{12,10},{14,12},{16,14},{18,16},{20... | collective-permute-start | bytes 1572872 | tf_op jit(solution)/shard_map/while/body/eval_jaxpr/ppermute | solution.py:19
  18.9 18.9 %collective-permute-start.1 = (f32[1024,128]{1,0:T(8,128)S(1)}, f32[1024,128]{1,0:T(8,128)}, u32[]{:S(2)}, u32[]{:S(2)}) collective-permute-start(f32[1024,128]{1,0:T(8,128)S(1)} %get-tuple-element.138), channel_id=1, source_target_pairs={{0,2},{2,4},{4,6},{6,8},{8,10},{10,12},{12,14},{14,16},{16,18},{18... | collective-permute-start | bytes 1572872 | tf_op jit(solution)/shard_map/while/body/eval_jaxpr/ppermute | solution.py:17
  30.0 0.8 copy-start.2
  74.5 62.2 %all-reduce.2.cloned.1.call-start = ((), (), s32[]{:S(2)}) async-start(), calls=%async_computation | async-start | bytes 2097152 | tf_op jit(solution)/shard_map/while/body/eval_jaxpr/pmax | solution.py:55
  74.6 19.1 %collective-permute-start = (f32[1024,128]{1,0:T(8,128)S(1)}, f32[1024,128]{1,0:T(8,128)S(1)}, u32[]{:S(2)}, u32[]{:S(2)}) collective-permute-start(f32[1024,128]{1,0:T(8,128)S(1)} %get-tuple-element.137), channel_id=1, source_target_pairs={{2,0},{4,2},{6,4},{8,6},{10,8},{12,10},{14,12},{16,14},{18,16},{20... | collective-permute-start | bytes 1572872 | tf_op jit(solution)/shard_map/while/body/eval_jaxpr/ppermute | solution.py:19
  82.0 19.4 %collective-permute-start.1 = (f32[1024,128]{1,0:T(8,128)S(1)}, f32[1024,128]{1,0:T(8,128)}, u32[]{:S(2)}, u32[]{:S(2)}) collective-permute-start(f32[1024,128]{1,0:T(8,128)S(1)} %get-tuple-element.138), channel_id=1, source_target_pairs={{0,2},{2,4},{4,6},{6,8},{8,10},{10,12},{12,14},{14,16},{16,18},{18... | collective-permute-start | bytes 1572872 | tf_op jit(solution)/shard_map/while/body/eval_jaxpr/ppermute | solution.py:17
  93.6 0.8 copy-start.2
  138.1 62.2 %all-reduce.2.cloned.1.call-start = ((), (), s32[]{:S(2)}) async-start(), calls=%async_computation | async-start | bytes 2097152 | tf_op jit(solution)/shard_map/while/body/eval_jaxpr/pmax | solution.py:55
  138.2 19.1 %collective-permute-start = (f32[1024,128]{1,0:T(8,128)S(1)}, f32[1024,128]{1,0:T(8,128)S(1)}, u32[]{:S(2)}, u32[]{:S(2)}) collective-permute-start(f32[1024,128]{1,0:T(8,128)S(1)} %get-tuple-element.137), channel_id=1, source_target_pairs={{2,0},{4,2},{6,4},{8,6},{10,8},{12,10},{14,12},{16,14},{18,16},{20... | collective-permute-start | bytes 1572872 | tf_op jit(solution)/shard_map/while/body/eval_jaxpr/ppermute | solution.py:19
  145.6 19.4 %collective-permute-start.1 = (f32[1024,128]{1,0:T(8,128)S(1)}, f32[1024,128]{1,0:T(8,128)}, u32[]{:S(2)}, u32[]{:S(2)}) collective-permute-start(f32[1024,128]{1,0:T(8,128)S(1)} %get-tuple-element.138), channel_id=1, source_target_pairs={{0,2},{2,4},{4,6},{6,8},{8,10},{10,12},{12,14},{14,16},{16,18},{18... | collective-permute-start | bytes 1572872 | tf_op jit(solution)/shard_map/while/body/eval_jaxpr/ppermute | solution.py:17
  157.2 0.8 copy-start.2
  201.6 62.2 %all-reduce.2.cloned.1.call-start = ((), (), s32[]{:S(2)}) async-start(), calls=%async_computation | async-start | bytes 2097152 | tf_op jit(solution)/shard_map/while/body/eval_jaxpr/pmax | solution.py:55
  201.8 19.1 %collective-permute-start = (f32[1024,128]{1,0:T(8,128)S(1)}, f32[1024,128]{1,0:T(8,128)S(1)}, u32[]{:S(2)}, u32[]{:S(2)}) collective-permute-start(f32[1024,128]{1,0:T(8,128)S(1)} %get-tuple-element.137), channel_id=1, source_target_pairs={{2,0},{4,2},{6,4},{8,6},{10,8},{12,10},{14,12},{16,14},{18,16},{20... | collective-permute-start | bytes 1572872 | tf_op jit(solution)/shard_map/while/body/eval_jaxpr/ppermute | solution.py:19
  209.2 19.4 %collective-permute-start.1 = (f32[1024,128]{1,0:T(8,128)S(1)}, f32[1024,128]{1,0:T(8,128)}, u32[]{:S(2)}, u32[]{:S(2)}) collective-permute-start(f32[1024,128]{1,0:T(8,128)S(1)} %get-tuple-element.138), channel_id=1, source_target_pairs={{0,2},{2,4},{4,6},{6,8},{8,10},{10,12},{12,14},{14,16},{16,18},{18... | collective-permute-start | bytes 1572872 | tf_op jit(solution)/shard_map/while/body/eval_jaxpr/ppermute | solution.py:17
  220.8 0.8 copy-start.2
  265.2 62.2 %all-reduce.2.cloned.1.call-start = ((), (), s32[]{:S(2)}) async-start(), calls=%async_computation | async-start | bytes 2097152 | tf_op jit(solution)/shard_map/while/body/eval_jaxpr/pmax | solution.py:55
  265.4 19.1 %collective-permute-start = (f32[1024,128]{1,0:T(8,128)S(1)}, f32[1024,128]{1,0:T(8,128)S(1)}, u32[]{:S(2)}, u32[]{:S(2)}) collective-permute-start(f32[1024,128]{1,0:T(8,128)S(1)} %get-tuple-element.137), channel_id=1, source_target_pairs={{2,0},{4,2},{6,4},{8,6},{10,8},{12,10},{14,12},{16,14},{18,16},{20... | collective-permute-start | bytes 1572872 | tf_op jit(solution)/shard_map/while/body/eval_jaxpr/ppermute | solution.py:19
  272.8 19.4 %collective-permute-start.1 = (f32[1024,128]{1,0:T(8,128)S(1)}, f32[1024,128]{1,0:T(8,128)}, u32[]{:S(2)}, u32[]{:S(2)}) collective-permute-start(f32[1024,128]{1,0:T(8,128)S(1)} %get-tuple-element.138), channel_id=1, source_target_pairs={{0,2},{2,4},{4,6},{6,8},{8,10},{10,12},{12,14},{14,16},{16,18},{18... | collective-permute-start | bytes 1572872 | tf_op jit(solution)/shard_map/while/body/eval_jaxpr/ppermute | solution.py:17
  284.4 0.8 copy-start.2
  328.8 62.2 %all-reduce.2.cloned.1.call-start = ((), (), s32[]{:S(2)}) async-start(), calls=%async_computation | async-start | bytes 2097152 | tf_op jit(solution)/shard_map/while/body/eval_jaxpr/pmax | solution.py:55
  329.0 19.1 %collective-permute-start = (f32[1024,128]{1,0:T(8,128)S(1)}, f32[1024,128]{1,0:T(8,128)S(1)}, u32[]{:S(2)}, u32[]{:S(2)}) collective-permute-start(f32[1024,128]{1,0:T(8,128)S(1)} %get-tuple-element.137), channel_id=1, source_target_pairs={{2,0},{4,2},{6,4},{8,6},{10,8},{12,10},{14,12},{16,14},{18,16},{20... | collective-permute-start | bytes 1572872 | tf_op jit(solution)/shard_map/while/body/eval_jaxpr/ppermute | solution.py:19
  336.4 19.4 %collective-permute-start.1 = (f32[1024,128]{1,0:T(8,128)S(1)}, f32[1024,128]{1,0:T(8,128)}, u32[]{:S(2)}, u32[]{:S(2)}) collective-permute-start(f32[1024,128]{1,0:T(8,128)S(1)} %get-tuple-element.138), channel_id=1, source_target_pairs={{0,2},{2,4},{4,6},{6,8},{8,10},{10,12},{12,14},{14,16},{16,18},{18... | collective-permute-start | bytes 1572872 | tf_op jit(solution)/shard_map/while/body/eval_jaxpr/ppermute | solution.py:17
  348.0 0.8 copy-start.2
  392.4 62.2 %all-reduce.2.cloned.1.call-start = ((), (), s32[]{:S(2)}) async-start(), calls=%async_computation | async-start | bytes 2097152 | tf_op jit(solution)/shard_map/while/body/eval_jaxpr/pmax | solution.py:55
  392.6 19.1 %collective-permute-start = (f32[1024,128]{1,0:T(8,128)S(1)}, f32[1024,128]{1,0:T(8,128)S(1)}, u32[]{:S(2)}, u32[]{:S(2)}) collective-permute-start(f32[1024,128]{1,0:T(8,128)S(1)} %get-tuple-element.137), channel_id=1, source_target_pairs={{2,0},{4,2},{6,4},{8,6},{10,8},{12,10},{14,12},{16,14},{18,16},{20... | collective-permute-start | bytes 1572872 | tf_op jit(solution)/shard_map/while/body/eval_jaxpr/ppermute | solution.py:19
  400.0 19.4 %collective-permute-start.1 = (f32[1024,128]{1,0:T(8,128)S(1)}, f32[1024,128]{1,0:T(8,128)}, u32[]{:S(2)}, u32[]{:S(2)}) collective-permute-start(f32[1024,128]{1,0:T(8,128)S(1)} %get-tuple-element.138), channel_id=1, source_target_pairs={{0,2},{2,4},{4,6},{6,8},{8,10},{10,12},{12,14},{14,16},{16,18},{18... | collective-permute-start | bytes 1572872 | tf_op jit(solution)/shard_map/while/body/eval_jaxpr/ppermute | solution.py:17
  411.6 0.8 copy-start.2
  456.0 62.2 %all-reduce.2.cloned.1.call-start = ((), (), s32[]{:S(2)}) async-start(), calls=%async_computation | async-start | bytes 2097152 | tf_op jit(solution)/shard_map/while/body/eval_jaxpr/pmax | solution.py:55
  456.1 19.1 %collective-permute-start = (f32[1024,128]{1,0:T(8,128)S(1)}, f32[1024,128]{1,0:T(8,128)S(1)}, u32[]{:S(2)}, u32[]{:S(2)}) collective-permute-start(f32[1024,128]{1,0:T(8,128)S(1)} %get-tuple-element.137), channel_id=1, source_target_pairs={{2,0},{4,2},{6,4},{8,6},{10,8},{12,10},{14,12},{16,14},{18,16},{20... | collective-permute-start | bytes 1572872 | tf_op jit(solution)/shard_map/while/body/eval_jaxpr/ppermute | solution.py:19
  463.6 19.4 %collective-permute-start.1 = (f32[1024,128]{1,0:T(8,128)S(1)}, f32[1024,128]{1,0:T(8,128)}, u32[]{:S(2)}, u32[]{:S(2)}) collective-permute-start(f32[1024,128]{1,0:T(8,128)S(1)} %get-tuple-element.138), channel_id=1, source_target_pairs={{0,2},{2,4},{4,6},{6,8},{8,10},{10,12},{12,14},{14,16},{16,18},{18... | collective-permute-start | bytes 1572872 | tf_op jit(solution)/shard_map/while/body/eval_jaxpr/ppermute | solution.py:17
  475.2 0.8 copy-start.2
  519.6 62.2 %all-reduce.2.cloned.1.call-start = ((), (), s32[]{:S(2)}) async-start(), calls=%async_computation | async-start | bytes 2097152 | tf_op jit(solution)/shard_map/while/body/eval_jaxpr/pmax | solution.py:55
  519.7 19.1 %collective-permute-start = (f32[1024,128]{1,0:T(8,128)S(1)}, f32[1024,128]{1,0:T(8,128)S(1)}, u32[]{:S(2)}, u32[]{:S(2)}) collective-permute-start(f32[1024,128]{1,0:T(8,128)S(1)} %get-tuple-element.137), channel_id=1, source_target_pairs={{2,0},{4,2},{6,4},{8,6},{10,8},{12,10},{14,12},{16,14},{18,16},{20... | collective-permute-start | bytes 1572872 | tf_op jit(solution)/shard_map/while/body/eval_jaxpr/ppermute | solution.py:19
  527.2 19.4 %collective-permute-start.1 = (f32[1024,128]{1,0:T(8,128)S(1)}, f32[1024,128]{1,0:T(8,128)}, u32[]{:S(2)}, u32[]{:S(2)}) collective-permute-start(f32[1024,128]{1,0:T(8,128)S(1)} %get-tuple-element.138), channel_id=1, source_target_pairs={{0,2},{2,4},{4,6},{6,8},{8,10},{10,12},{12,14},{14,16},{16,18},{18... | collective-permute-start | bytes 1572872 | tf_op jit(solution)/shard_map/while/body/eval_jaxpr/ppermute | solution.py:17
  538.8 0.8 copy-start.2
  583.2 62.2 %all-reduce.2.cloned.1.call-start = ((), (), s32[]{:S(2)}) async-start(), calls=%async_computation | async-start | bytes 2097152 | tf_op jit(solution)/shard_map/while/body/eval_jaxpr/pmax | solution.py:55
  583.3 19.1 %collective-permute-start = (f32[1024,128]{1,0:T(8,128)S(1)}, f32[1024,128]{1,0:T(8,128)S(1)}, u32[]{:S(2)}, u32[]{:S(2)}) collective-permute-start(f32[1024,128]{1,0:T(8,128)S(1)} %get-tuple-element.137), channel_id=1, source_target_pairs={{2,0},{4,2},{6,4},{8,6},{10,8},{12,10},{14,12},{16,14},{18,16},{20... | collective-permute-start | bytes 1572872 | tf_op jit(solution)/shard_map/while/body/eval_jaxpr/ppermute | solution.py:19
  590.8 19.4 %collective-permute-start.1 = (f32[1024,128]{1,0:T(8,128)S(1)}, f32[1024,128]{1,0:T(8,128)}, u32[]{:S(2)}, u32[]{:S(2)}) collective-permute-start(f32[1024,128]{1,0:T(8,128)S(1)} %get-tuple-element.138), channel_id=1, source_target_pairs={{0,2},{2,4},{4,6},{6,8},{8,10},{10,12},{12,14},{14,16},{16,18},{18... | collective-permute-start | bytes 1572872 | tf_op jit(solution)/shard_map/while/body/eval_jaxpr/ppermute | solution.py:17
  602.4 0.8 copy-start.2
  646.8 62.2 %all-reduce.2.cloned.1.call-start = ((), (), s32[]{:S(2)}) async-start(), calls=%async_computation | async-start | bytes 2097152 | tf_op jit(solution)/shard_map/while/body/eval_jaxpr/pmax | solution.py:55
  646.9 19.1 %collective-permute-start = (f32[1024,128]{1,0:T(8,128)S(1)}, f32[1024,128]{1,0:T(8,128)S(1)}, u32[]{:S(2)}, u32[]{:S(2)}) collective-permute-start(f32[1024,128]{1,0:T(8,128)S(1)} %get-tuple-element.137), channel_id=1, source_target_pairs={{2,0},{4,2},{6,4},{8,6},{10,8},{12,10},{14,12},{16,14},{18,16},{20... | collective-permute-start | bytes 1572872 | tf_op jit(solution)/shard_map/while/body/eval_jaxpr/ppermute | solution.py:19
  654.3 19.4 %collective-permute-start.1 = (f32[1024,128]{1,0:T(8,128)S(1)}, f32[1024,128]{1,0:T(8,128)}, u32[]{:S(2)}, u32[]{:S(2)}) collective-permute-start(f32[1024,128]{1,0:T(8,128)S(1)} %get-tuple-element.138), channel_id=1, source_target_pairs={{0,2},{2,4},{4,6},{6,8},{8,10},{10,12},{12,14},{14,16},{16,18},{18... | collective-permute-start | bytes 1572872 | tf_op jit(solution)/shard_map/while/body/eval_jaxpr/ppermute | solution.py:17
  666.0 0.8 copy-start.2
  710.4 62.2 %all-reduce.2.cloned.1.call-start = ((), (), s32[]{:S(2)}) async-start(), calls=%async_computation | async-start | bytes 2097152 | tf_op jit(solution)/shard_map/while/body/eval_jaxpr/pmax | solution.py:55
  710.5 19.1 %collective-permute-start = (f32[1024,128]{1,0:T(8,128)S(1)}, f32[1024,128]{1,0:T(8,128)S(1)}, u32[]{:S(2)}, u32[]{:S(2)}) collective-permute-start(f32[1024,128]{1,0:T(8,128)S(1)} %get-tuple-element.137), channel_id=1, source_target_pairs={{2,0},{4,2},{6,4},{8,6},{10,8},{12,10},{14,12},{16,14},{18,16},{20... | collective-permute-start | bytes 1572872 | tf_op jit(solution)/shard_map/while/body/eval_jaxpr/ppermute | solution.py:19
  717.9 19.4 %collective-permute-start.1 = (f32[1024,128]{1,0:T(8,128)S(1)}, f32[1024,128]{1,0:T(8,128)}, u32[]{:S(2)}, u32[]{:S(2)}) collective-permute-start(f32[1024,128]{1,0:T(8,128)S(1)} %get-tuple-element.138), channel_id=1, source_target_pairs={{0,2},{2,4},{4,6},{6,8},{8,10},{10,12},{12,14},{14,16},{16,18},{18... | collective-permute-start | bytes 1572872 | tf_op jit(solution)/shard_map/while/body/eval_jaxpr/ppermute | solution.py:17
  774.0 1.0 copy-start.1
  (2 other events, 1.5 us)
Sparse Core Ops, SparseCore 0:
  53.7 19.3 all-reduce.1
  117.3 19.3 all-reduce.1
  180.9 19.3 all-reduce.1
  244.5 19.3 all-reduce.1
  308.1 19.3 all-reduce.1
  371.6 19.3 all-reduce.1
  435.2 19.3 all-reduce.1
  498.8 19.3 all-reduce.1
  562.4 19.3 all-reduce.1
  626.0 19.3 all-reduce.1
  689.6 19.3 all-reduce.1
  753.2 19.3 all-reduce.1
where the time goes:
time: 784 us; the launch traced here: 782 us
  waiting for transfers between devices  454 us (58%)
  matrix products  124 us (16%)
  starting transfers between devices  91 us (12%)
  local copies, waits for them, and re-layouts  63.1 us (8%)
  other arithmetic  34.9 us (4%)
  between operations  13.4 us (2%)
    pmax x12, waiting for transfers between devices, action_sweep(): merged = lax.pmax(largest, 'act')  235 us
    ppermute x12, waiting for transfers between devices, extended(): lax.ppermute(head, axis, [((i + 1) % count, i) for i in range(count)])  136 us
    dot_general x12, matrix products, products(): jnp.einsum('arbij,arbjk->arik', tiles, picked, precision=lax.Precision.HI...  124 us
    ppermute x12, starting transfers between devices, extended(): lax.ppermute(head, axis, [((i + 1) % count, i) for i in range(count)])  90.5 us
    ppermute x12, waiting for transfers between devices, extended(): lax.ppermute(tail, axis, [(i, (i + 1) % count) for i in range(count)])  83.3 us
    gather x12, local copies, waits for them, and re-layouts, products(): picked = blocks[local_index]  33 us
    concatenate x12, other arithmetic, extended(): jnp.concatenate([lax.ppermute(tail, axis, [(i, (i + 1) % count) for i in...  16 us
    select_n x12, other arithmetic, action_sweep(): jnp.where(target_hit, jnp.float32(1.0), merged.reshape(-1, target_sets))  15.9 us
  transfers between devices with their start and end apart: 36, of which 36 were waited for; matrix products, arithmetic and copies ran while one was open for 0% of the time, Pallas kernels for 0%

commit v1 on v0

v1 whole, which is shorter than its diff:
```python
import functools

import jax
import jax.numpy as jnp
from jax import lax
from jax.experimental import pallas as pl
from jax.experimental.pallas import tpu as pltpu
from jax.sharding import PartitionSpec as P

REACH = 8
SWEEPS = 12
MESH = pl.DeviceIdType.MESH


def sweep_kernel(n_states, pos_ref, trans_hbm, tgt_ref, out_ref,
                 win0, win1, t_own, t_oth, tsem, send_sem, recv_sem):
    i = lax.axis_index("states")
    c = lax.axis_index("act")
    half = t_own.shape[1]
    tile = t_own.shape[3]
    own_pos = half + half * c
    part_pos = 2 * half - half * c
    halo_pos = 3 * half * c
    nb_halo_pos = 3 * half * (1 - c)
    partner = (i, 1 - c)
    neighbour = (lax.rem(i + 2 * c - 1 + n_states, n_states), 1 - c)

    barrier = pltpu.get_barrier_semaphore()
    for dev in (partner, neighbour):
        pl.semaphore_signal(barrier, inc=1, device_id=dev, device_id_type=MESH)
    pl.semaphore_wait(barrier, 2)

    own_copy = pltpu.make_async_copy(trans_hbm.at[:, pl.ds(half * c, half)], t_own, tsem.at[0])
    own_copy.start()
    oth_copy = pltpu.make_async_remote_copy(
        src_ref=trans_hbm.at[:, pl.ds(half * (1 - c), half)], dst_ref=t_oth,
        send_sem=tsem.at[1], recv_sem=tsem.at[2], device_id=partner, device_id_type=MESH)
    oth_copy.start()

    win0[pl.ds(half, 2 * half)] = tgt_ref[...].astype(jnp.float32)
    init = pltpu.make_async_remote_copy(
        src_ref=win0.at[pl.ds(own_pos, half)], dst_ref=win0.at[pl.ds(nb_halo_pos, half)],
        send_sem=send_sem.at[0, 1], recv_sem=recv_sem.at[0, 1],
        device_id=neighbour, device_id_type=MESH)
    init.start()
    init.wait_send()
    init.wait_recv()
    own_copy.wait()
    oth_copy.wait_send()
    oth_copy.wait_recv()

    def sweep(src, dst, slot):
        def block(jj, carry):
            j = half * c + jj
            best = None
            for tv, base in ((t_own, 2 * c), (t_oth, 2 * (1 - c))):
                for al in range(tv.shape[0]):
                    a = base + al
                    q = None
                    for t in range(tv.shape[2]):
                        v = src[pos_ref[a, j, t]]
                        p = jnp.dot(tv[al, jj, t], v, precision=lax.Precision.HIGHEST,
                                    preferred_element_type=jnp.float32)
                        q = p if q is None else q + p
                    best = q if best is None else jnp.maximum(best, q)
            dst[own_pos + jj] = jnp.where(tgt_ref[j] == 1, jnp.float32(1.0), best)
            return carry

        lax.fori_loop(0, half, block, 0)
        to_partner = pltpu.make_async_remote_copy(
            src_ref=dst.at[pl.ds(own_pos, half)], dst_ref=dst.at[pl.ds(own_pos, half)],
            send_sem=send_sem.at[slot, 0], recv_sem=recv_sem.at[slot, 0],
            device_id=partner, device_id_type=MESH)
        to_neighbour = pltpu.make_async_remote_copy(
            src_ref=dst.at[pl.ds(own_pos, half)], dst_ref=dst.at[pl.ds(nb_halo_pos, half)],
            send_sem=send_sem.at[slot, 1], recv_sem=recv_sem.at[slot, 1],
            device_id=neighbour, device_id_type=MESH)
        to_partner.start()
        to_neighbour.start()
        to_partner.wait_send()
        to_neighbour.wait_send()
        to_partner.wait_recv()
        to_neighbour.wait_recv()

    def pair(k, carry):
        sweep(win0, win1, 1)
        sweep(win1, win0, 0)
        return carry

    lax.fori_loop(0, SWEEPS // 2, pair, 0)
    out_ref[...] = win0[pl.ds(half, 2 * half)]


def per_device(transitions, columns, targets):
    n_states = lax.axis_size("states")
    rb = transitions.shape[1]
    tile = transitions.shape[3]
    ksets = targets.shape[1]
    total_blocks = rb * n_states
    first = lax.axis_index("states") * rb - REACH
    pos = lax.rem(columns - first + 2 * total_blocks, total_blocks).astype(jnp.int32)
    tgt = targets.reshape(rb, tile, ksets)
    half = rb // 2
    out = pl.pallas_call(
        functools.partial(sweep_kernel, n_states),
        out_shape=jax.ShapeDtypeStruct((rb, tile, ksets), jnp.float32),
        in_specs=[
            pl.BlockSpec(memory_space=pltpu.SMEM),
            pl.BlockSpec(memory_space=pl.ANY),
            pl.BlockSpec(memory_space=pltpu.VMEM),
        ],
        out_specs=pl.BlockSpec(memory_space=pltpu.VMEM),
        scratch_shapes=[
            pltpu.VMEM((rb + 2 * REACH, tile, ksets), jnp.float32),
            pltpu.VMEM((rb + 2 * REACH, tile, ksets), jnp.float32),
            pltpu.VMEM((transitions.shape[0], half) + transitions.shape[2:], jnp.float32),
            pltpu.VMEM((transitions.shape[0], half) + transitions.shape[2:], jnp.float32),
            pltpu.SemaphoreType.DMA((3,)),
            pltpu.SemaphoreType.DMA((2, 2)),
            pltpu.SemaphoreType.DMA((2, 2)),
        ],
        compiler_params=pltpu.CompilerParams(
            collective_id=0, has_side_effects=True, vmem_limit_bytes=48 * 1024 * 1024),
    )(pos, transitions, tgt)
    return out.reshape(rb * tile, ksets)


def solution(mesh):
    return jax.shard_map(
        per_device,
        mesh=mesh,
        in_specs=(P("act", "states", None, None, None), P(None, "states", None), P("states", None)),
        out_specs=P("states", None),
        check_vma=False,
    )
```

time: 784 us -> 203 us (0.26)
  waiting for transfers between devices: 454 us -> 0 us
  Pallas kernels: 0 us -> 200 us
  matrix products: 124 us -> 0 us
  starting transfers between devices: 91 us -> 0 us
  local copies, waits for them, and re-layouts: 63.1 us -> 2.3 us
  other arithmetic: 34.9 us -> 0.7 us
  between operations: 13.4 us -> 0.02 us
    pmax x12 -> x0, waiting for transfers between devices: 235 us -> none  [action_sweep(): merged = lax.pmax(largest, 'act')]
    ppermute x24 -> x0, waiting for transfers between devices: 220 us -> none  [the longest x12 136 us: extended(): lax.ppermute(head, axis, [((i + 1) % count, i) for i in range(count)])]
    pallas_call x0 -> x1, Pallas kernels: none -> 200 us  [per_device(): pl.pallas_call(functools.partial(sweep_kernel, n_states), out_shape=jax.S...]
    dot_general x12 -> x0, matrix products: 124 us -> none  [products(): jnp.einsum('arbij,arbjk->arik', tiles, picked, precision=lax.Precision.HI...]
    ppermute x24 -> x0, starting transfers between devices: 90.5 us -> none  [the longest x12 90.5 us: extended(): lax.ppermute(head, axis, [((i + 1) % count, i) for i in range(count)])]
    gather x12 -> x0, local copies, waits for them, and re-layouts: 33 us -> none  [products(): picked = blocks[local_index]]
    select_n x24 -> x0, other arithmetic: 16.1 us -> none  [the longest x12 15.9 us: action_sweep(): jnp.where(target_hit, jnp.float32(1.0), merged.reshape(-1, target_sets))]
    concatenate x12 -> x0, other arithmetic: 16 us -> none  [extended(): jnp.concatenate([lax.ppermute(tail, axis, [(i, (i + 1) % count) for i in...]
  transfers between devices with their start and end apart: 36 -> 0, of which waited for: 36 -> 0; matrix products, arithmetic and copies ran while one was open for 0% -> 0% of each run, Pallas kernels for 0% -> 0%
where the time goes in v1:
time: 203 us
  Pallas kernels  200 us (99%)
  local copies, waits for them, and re-layouts  2.3 us (1%)
    pallas_call x1, Pallas kernels, per_device(): pl.pallas_call(functools.partial(sweep_kernel, n_states), out_shape=jax.S...  200 us

profile of v1, /device:TPU:0, one launch (start us, length us, event | category | flops | bytes accessed | tf_op | source)
XLA Modules:
  0.0 202.9 jit_solution(814512351245129336)
XLA Ops:
  0.0 0.7 broadcast_subtract_fusion
  0.7 0.1 copy.7
  0.8 0.0 copy-start
  0.8 1.2 copy-done
  2.0 199.9 %shard_map.37 = f32[16,128,128]{2,1,0:T(8,128)S(1)} custom-call(s32[4,16,2]{2,1,0:T(8,128)S(1)} %negate_select_fusion.pos_ref, f32[2,16,2,128,128]{4,3,2,1,0:T(8,128)} %trans_hbm.1, s32[16,128,128]{2,1,0:T(8,128)S(1)} %bitcast.5), custom_call_target="tpu_custom_call" | custom-call | tf_op jit(solution)/shard_map/pallas_call | solution.py:104
  202.0 1.0 copy.9
  (1 shorter events, 0.0 us)
Async XLA Ops:
  0.8 1.2 copy-start

commit v2 on v1

--- a/solution.py
+++ b/solution.py
@@ -12,10 +12,23 @@
 MESH = pl.DeviceIdType.MESH
 
 
+def split_blocks(src, hi, lo, first, count):
+    def body(k, carry):
+        v = src[first + k]
+        h = v.astype(jnp.bfloat16)
+        hi[first + k] = h
+        lo[first + k] = (v - h.astype(jnp.float32)).astype(jnp.bfloat16)
+        return carry
+
+    lax.fori_loop(0, count, body, 0)
+
+
 def sweep_kernel(n_states, pos_ref, trans_hbm, tgt_ref, out_ref,
-                 win0, win1, t_own, t_oth, tsem, send_sem, recv_sem):
+                 win0, win1, hi0, hi1, lo0, lo1, t_own, t_oth, thi, tlo,
+                 tsem, send_sem, recv_sem):
     i = lax.axis_index("states")
     c = lax.axis_index("act")
+    acts = t_own.shape[0]
     half = t_own.shape[1]
     tile = t_own.shape[3]
     own_pos = half + half * c
@@ -43,27 +56,60 @@
         send_sem=send_sem.at[0, 1], recv_sem=recv_sem.at[0, 1],
         device_id=neighbour, device_id_type=MESH)
     init.start()
+    split_blocks(win0, hi0, lo0, half, 2 * half)
+
+    def prep(tv, first):
+        def body(k, carry):
+            al = k // half
+            jj = k % half
+            for t in range(tv.shape[2]):
+                v = tv[al, jj, t]
+                h = v.astype(jnp.bfloat16)
+                thi[first + al, jj, :, pl.ds(t * tile, tile)] = h
+                tlo[first + al, jj, :, pl.ds(t * tile, tile)] = (
+                    v - h.astype(jnp.float32)).astype(jnp.bfloat16)
+            return carry
+
+        lax.fori_loop(0, acts * half, body, 0)
+
+    own_copy.wait()
+    prep(t_own, 0)
+    oth_copy.wait_send()
+    oth_copy.wait_recv()
+    prep(t_oth, acts)
     init.wait_send()
     init.wait_recv()
-    own_copy.wait()
-    oth_copy.wait_send()
-    oth_copy.wait_recv()
+    split_blocks(win0, hi0, lo0, halo_pos, half)
 
-    def sweep(src, dst, slot):
+    def sweep(src_hi, src_lo, dst, dst_hi, dst_lo, slot):
         def block(jj, carry):
             j = half * c + jj
             best = None
-            for tv, base in ((t_own, 2 * c), (t_oth, 2 * (1 - c))):
-                for al in range(tv.shape[0]):
-                    a = base + al
-                    q = None
-                    for t in range(tv.shape[2]):
-                        v = src[pos_ref[a, j, t]]
-                        p = jnp.dot(tv[al, jj, t], v, precision=lax.Precision.HIGHEST,
-                                    preferred_element_type=jnp.float32)
-                        q = p if q is None else q + p
-                    best = q if best is None else jnp.maximum(best, q)
-            dst[own_pos + jj] = jnp.where(tgt_ref[j] == 1, jnp.float32(1.0), best)
+            for ab in range(2 * acts):
+                a = lax.rem(2 * c + ab, 2 * acts)
+                p0 = pos_ref[a, j, 0]
+                p1 = pos_ref[a, j, 1]
+                vh = jnp.concatenate([src_hi[p0], src_hi[p1]], axis=0)
+                vl = jnp.concatenate([src_lo[p0], src_lo[p1]], axis=0)
+                th = thi[ab, jj]
+                tl = tlo[ab, jj]
+                q = jnp.dot(th, vh, preferred_element_type=jnp.float32)
+                q = q + jnp.dot(th, vl, preferred_element_type=jnp.float32)
+                q = q + jnp.dot(tl, vh, preferred_element_type=jnp.float32)
+                best = q if best is None else jnp.maximum(best, q)
+            val = jnp.where(tgt_ref[j] == 1, jnp.float32(1.0), best)
+            dst[own_pos + jj] = val
+            h = val.astype(jnp.bfloat16)
+            dst_hi[own_pos + jj] = h
+            dst_lo[own_pos + jj] = (val - h.astype(jnp.float32)).astype(jnp.bfloat16)
+            pltpu.make_async_remote_copy(
+                src_ref=dst.at[own_pos + jj], dst_ref=dst.at[own_pos + jj],
+                send_sem=send_sem.at[slot, 0], recv_sem=recv_sem.at[slot, 0],
+                device_id=partner, device_id_type=MESH).start()
+            pltpu.make_async_remote_copy(
+                src_ref=dst.at[own_pos + jj], dst_ref=dst.at[nb_halo_pos + jj],
+                send_sem=send_sem.at[slot, 1], recv_sem=recv_sem.at[slot, 1],
+                device_id=neighbour, device_id_type=MESH).start()
             return carry
 
         lax.fori_loop(0, half, block, 0)
@@ -75,16 +121,16 @@
             src_ref=dst.at[pl.ds(own_pos, half)], dst_ref=dst.at[pl.ds(nb_halo_pos, half)],
             send_sem=send_sem.at[slot, 1], recv_sem=recv_sem.at[slot, 1],
             device_id=neighbour, device_id_type=MESH)
-        to_partner.start()
-        to_neighbour.start()
         to_partner.wait_send()
         to_neighbour.wait_send()
         to_partner.wait_recv()
+        split_blocks(dst, dst_hi, dst_lo, part_pos, half)
         to_neighbour.wait_recv()
+        split_blocks(dst, dst_hi, dst_lo, halo_pos, half)
 
     def pair(k, carry):
-        sweep(win0, win1, 1)
-        sweep(win1, win0, 0)
+        sweep(hi0, lo0, win1, hi1, lo1, 1)
+        sweep(hi1, lo1, win0, hi0, lo0, 0)
         return carry
 
     lax.fori_loop(0, SWEEPS // 2, pair, 0)
@@ -113,8 +159,14 @@
         scratch_shapes=[
             pltpu.VMEM((rb + 2 * REACH, tile, ksets), jnp.float32),
             pltpu.VMEM((rb + 2 * REACH, tile, ksets), jnp.float32),
+            pltpu.VMEM((rb + 2 * REACH, tile, ksets), jnp.bfloat16),
+            pltpu.VMEM((rb + 2 * REACH, tile, ksets), jnp.bfloat16),
+            pltpu.VMEM((rb + 2 * REACH, tile, ksets), jnp.bfloat16),
+            pltpu.VMEM((rb + 2 * REACH, tile, ksets), jnp.bfloat16),
             pltpu.VMEM((transitions.shape[0], half) + transitions.shape[2:], jnp.float32),
             pltpu.VMEM((transitions.shape[0], half) + transitions.shape[2:], jnp.float32),
+            pltpu.VMEM((2 * transitions.shape[0], half, tile, 2 * tile), jnp.bfloat16),
+            pltpu.VMEM((2 * transitions.shape[0], half, tile, 2 * tile), jnp.bfloat16),
             pltpu.SemaphoreType.DMA((3,)),
             pltpu.SemaphoreType.DMA((2, 2)),
             pltpu.SemaphoreType.DMA((2, 2)),

time: 203 us -> 151 us (0.74)
  Pallas kernels: 200 us -> 148 us
    pallas_call x1, Pallas kernels: 200 us -> 148 us  [per_device(): pl.pallas_call(functools.partial(sweep_kernel, n_states), out_shape=jax.S...]
where the time goes in v2:
time: 151 us
  Pallas kernels  148 us (98%)
  local copies, waits for them, and re-layouts  2.3 us (2%)
    pallas_call x1, Pallas kernels, per_device(): pl.pallas_call(functools.partial(sweep_kernel, n_states), out_shape=jax.S...  148 us

profile of v2, /device:TPU:0, one launch (start us, length us, event | category | flops | bytes accessed | tf_op | source)
XLA Modules:
  0.0 151.1 jit_solution(2622661253245178401)
XLA Ops:
  0.0 0.7 broadcast_subtract_fusion
  0.7 0.1 copy.7
  0.8 0.0 copy-start
  0.8 1.2 copy-done
  2.0 148.1 %shard_map.37 = f32[16,128,128]{2,1,0:T(8,128)S(1)} custom-call(s32[4,16,2]{2,1,0:T(8,128)S(1)} %negate_select_fusion.pos_ref, f32[2,16,2,128,128]{4,3,2,1,0:T(8,128)} %trans_hbm.1, s32[16,128,128]{2,1,0:T(8,128)S(1)} %bitcast.5), custom_call_target="tpu_custom_call" | custom-call | tf_op jit(solution)/shard_map/pallas_call | solution.py:150
  150.1 1.0 copy.9
  (1 shorter events, 0.0 us)
Async XLA Ops:
  0.8 1.2 copy-start

commit v3 on v2

--- a/solution.py
+++ b/solution.py
@@ -81,7 +81,7 @@
     init.wait_recv()
     split_blocks(win0, hi0, lo0, halo_pos, half)
 
-    def sweep(src_hi, src_lo, dst, dst_hi, dst_lo, slot):
+    def sweep(src_hi, src_lo, dst, dst_hi, dst_lo, slot, halo=True):
         def block(jj, carry):
             j = half * c + jj
             best = None
@@ -106,10 +106,11 @@
                 src_ref=dst.at[own_pos + jj], dst_ref=dst.at[own_pos + jj],
                 send_sem=send_sem.at[slot, 0], recv_sem=recv_sem.at[slot, 0],
                 device_id=partner, device_id_type=MESH).start()
-            pltpu.make_async_remote_copy(
-                src_ref=dst.at[own_pos + jj], dst_ref=dst.at[nb_halo_pos + jj],
-                send_sem=send_sem.at[slot, 1], recv_sem=recv_sem.at[slot, 1],
-                device_id=neighbour, device_id_type=MESH).start()
+            if halo:
+                pltpu.make_async_remote_copy(
+                    src_ref=dst.at[own_pos + jj], dst_ref=dst.at[nb_halo_pos + jj],
+                    send_sem=send_sem.at[slot, 1], recv_sem=recv_sem.at[slot, 1],
+                    device_id=neighbour, device_id_type=MESH).start()
             return carry
 
         lax.fori_loop(0, half, block, 0)
@@ -122,8 +123,10 @@
             send_sem=send_sem.at[slot, 1], recv_sem=recv_sem.at[slot, 1],
             device_id=neighbour, device_id_type=MESH)
         to_partner.wait_send()
+        to_partner.wait_recv()
+        if not halo:
+            return
         to_neighbour.wait_send()
-        to_partner.wait_recv()
         split_blocks(dst, dst_hi, dst_lo, part_pos, half)
         to_neighbour.wait_recv()
         split_blocks(dst, dst_hi, dst_lo, halo_pos, half)
@@ -133,7 +136,9 @@
         sweep(hi1, lo1, win0, hi0, lo0, 0)
         return carry
 
-    lax.fori_loop(0, SWEEPS // 2, pair, 0)
+    lax.fori_loop(0, SWEEPS // 2 - 1, pair, 0)
+    sweep(hi0, lo0, win1, hi1, lo1, 1)
+    sweep(hi1, lo1, win0, hi0, lo0, 0, halo=False)
     out_ref[...] = win0[pl.ds(half, 2 * half)]
 
 

time: 151 us -> 148 us (0.980)
  Pallas kernels: 148 us -> 144 us
    pallas_call x1, Pallas kernels: 148 us -> 144 us  [per_device(): pl.pallas_call(functools.partial(sweep_kernel, n_states), out_shape=jax.S...]
where the time goes in v3:
time: 148 us; the launch traced here: 147 us
  Pallas kernels  144 us (97%)
  local copies, waits for them, and re-layouts  2.3 us (2%)
    pallas_call x1, Pallas kernels, per_device(): pl.pallas_call(functools.partial(sweep_kernel, n_states), out_shape=jax.S...  144 us

profile of v3, /device:TPU:0, one launch (start us, length us, event | category | flops | bytes accessed | tf_op | source)
XLA Modules:
  0.0 146.9 jit_solution(4132276282953593921)
XLA Ops:
  0.0 0.7 broadcast_subtract_fusion
  0.7 0.1 copy.7
  0.8 0.0 copy-start
  0.8 1.2 copy-done
  2.0 143.9 %shard_map.37 = f32[16,128,128]{2,1,0:T(8,128)S(1)} custom-call(s32[4,16,2]{2,1,0:T(8,128)S(1)} %negate_select_fusion.pos_ref, f32[2,16,2,128,128]{4,3,2,1,0:T(8,128)} %trans_hbm.1, s32[16,128,128]{2,1,0:T(8,128)S(1)} %bitcast.5), custom_call_target="tpu_custom_call" | custom-call | tf_op jit(solution)/shard_map/pallas_call | solution.py:155
  146.0 1.0 copy.9
  (1 shorter events, 0.0 us)
Async XLA Ops:
  0.8 1.2 copy-start

commit v4 on v2

v4 whole, which is shorter than its diff:
```python
import functools

import jax
import jax.numpy as jnp
from jax import lax
from jax.experimental import pallas as pl
from jax.experimental.pallas import tpu as pltpu
from jax.sharding import PartitionSpec as P

REACH = 8
SWEEPS = 12
HALVES = 2
MESH = pl.DeviceIdType.MESH


def split_blocks(src, hi, lo, h, first, count):
    def body(k, carry):
        v = src[h, first + k]
        b = v.astype(jnp.bfloat16)
        hi[h, first + k] = b
        lo[h, first + k] = (v - b.astype(jnp.float32)).astype(jnp.bfloat16)
        return carry

    lax.fori_loop(0, count, body, 0)


def sweep_kernel(n_states, pos_ref, trans_hbm, tgt_ref, out_ref,
                 win0, win1, hi0, hi1, lo0, lo1, t_own, t_oth, thi, tlo,
                 tsem, send_sem, recv_sem):
    i = lax.axis_index("states")
    c = lax.axis_index("act")
    acts = t_own.shape[0]
    half = t_own.shape[1]
    tile = t_own.shape[3]
    own_pos = half + half * c
    part_pos = 2 * half - half * c
    halo_pos = 3 * half * c
    nb_halo_pos = 3 * half * (1 - c)
    partner = (i, 1 - c)
    neighbour = (lax.rem(i + 2 * c - 1 + n_states, n_states), 1 - c)
    wins = (win0, win1)
    his = (hi0, hi1)
    los = (lo0, lo1)

    barrier = pltpu.get_barrier_semaphore()
    for dev in (partner, neighbour):
        pl.semaphore_signal(barrier, inc=1, device_id=dev, device_id_type=MESH)
    pl.semaphore_wait(barrier, 2)

    def copy_to(slot, h, k, start, count, dst_start):
        dev = partner if k == 0 else neighbour
        return pltpu.make_async_remote_copy(
            src_ref=wins[slot].at[h, pl.ds(start, count)],
            dst_ref=wins[slot].at[h, pl.ds(dst_start, count)],
            send_sem=send_sem.at[slot, h, k], recv_sem=recv_sem.at[slot, h, k],
            device_id=dev, device_id_type=MESH)

    for h in range(HALVES):
        win0[h, pl.ds(half, 2 * half)] = tgt_ref[h].astype(jnp.float32)
        copy_to(0, h, 1, own_pos, half, nb_halo_pos).start()

    own_copy = pltpu.make_async_copy(trans_hbm.at[:, pl.ds(half * c, half)], t_own, tsem.at[0])
    own_copy.start()
    oth_copy = pltpu.make_async_remote_copy(
        src_ref=trans_hbm.at[:, pl.ds(half * (1 - c), half)], dst_ref=t_oth,
        send_sem=tsem.at[1], recv_sem=tsem.at[2], device_id=partner, device_id_type=MESH)
    oth_copy.start()
    for h in range(HALVES):
        split_blocks(win0, hi0, lo0, h, half, 2 * half)

    def prep(tv, first):
        def body(k, carry):
            al = k // half
            jj = k % half
            for t in range(tv.shape[2]):
                v = tv[al, jj, t]
                b = v.astype(jnp.bfloat16)
                thi[first + al, jj, :, pl.ds(t * tile, tile)] = b
                tlo[first + al, jj, :, pl.ds(t * tile, tile)] = (
                    v - b.astype(jnp.float32)).astype(jnp.bfloat16)
            return carry

        lax.fori_loop(0, acts * half, body, 0)

    own_copy.wait()
    prep(t_own, 0)
    oth_copy.wait_send()
    oth_copy.wait_recv()
    prep(t_oth, acts)

    def stage(h, src, dst, first=False, halo=True):
        if first:
            done = copy_to(src, h, 1, own_pos, half, halo_pos)
            done.wait_send()
            done.wait_recv()
            split_blocks(wins[src], his[src], los[src], h, halo_pos, half)
        else:
            for k, start in ((0, part_pos), (1, halo_pos)):
                done = copy_to(src, h, k, own_pos, half, start)
                done.wait_send()
                done.wait_recv()
                split_blocks(wins[src], his[src], los[src], h, start, half)
        src_hi, src_lo = his[src], los[src]
        dst_win, dst_hi, dst_lo = wins[dst], his[dst], los[dst]

        def block(jj, carry):
            j = half * c + jj
            best = None
            for ab in range(2 * acts):
                a = lax.rem(2 * c + ab, 2 * acts)
                p0 = pos_ref[a, j, 0]
                p1 = pos_ref[a, j, 1]
                vh = jnp.concatenate([src_hi[h, p0], src_hi[h, p1]], axis=0)
                vl = jnp.concatenate([src_lo[h, p0], src_lo[h, p1]], axis=0)
                th = thi[ab, jj]
                tl = tlo[ab, jj]
                q = jnp.dot(th, vh, preferred_element_type=jnp.float32)
                q = q + jnp.dot(th, vl, preferred_element_type=jnp.float32)
                q = q + jnp.dot(tl, vh, preferred_element_type=jnp.float32)
                best = q if best is None else jnp.maximum(best, q)
            val = jnp.where(tgt_ref[h, j] == 1, jnp.float32(1.0), best)
            dst_win[h, own_pos + jj] = val
            b = val.astype(jnp.bfloat16)
            dst_hi[h, own_pos + jj] = b
            dst_lo[h, own_pos + jj] = (val - b.astype(jnp.float32)).astype(jnp.bfloat16)
            copy_to(dst, h, 0, own_pos + jj, 1, own_pos + jj).start()
            if halo:
                copy_to(dst, h, 1, own_pos + jj, 1, nb_halo_pos + jj).start()
            return carry

        lax.fori_loop(0, half, block, 0)

    for h in range(HALVES):
        stage(h, 0, 1, first=True)

    def pair(k, carry):
        for h in range(HALVES):
            stage(h, 1, 0)
        for h in range(HALVES):
            stage(h, 0, 1)
        return carry

    lax.fori_loop(0, SWEEPS // 2 - 1, pair, 0)
    for h in range(HALVES):
        stage(h, 1, 0, halo=False)
    for h in range(HALVES):
        done = copy_to(0, h, 0, own_pos, half, part_pos)
        done.wait_send()
        done.wait_recv()
        out_ref[h] = win0[h, pl.ds(half, 2 * half)]


def per_device(transitions, columns, targets):
    n_states = lax.axis_size("states")
    rb = transitions.shape[1]
    tile = transitions.shape[3]
    ksets = targets.shape[1]
    kh = ksets // HALVES
    total_blocks = rb * n_states
    first = lax.axis_index("states") * rb - REACH
    pos = lax.rem(columns - first + 2 * total_blocks, total_blocks).astype(jnp.int32)
    tgt = targets.reshape(rb, tile, HALVES, kh).transpose(2, 0, 1, 3)
    half = rb // 2
    wshape = (HALVES, rb + 2 * REACH, tile, kh)
    out = pl.pallas_call(
        functools.partial(sweep_kernel, n_states),
        out_shape=jax.ShapeDtypeStruct((HALVES, rb, tile, kh), jnp.float32),
        in_specs=[
            pl.BlockSpec(memory_space=pltpu.SMEM),
            pl.BlockSpec(memory_space=pl.ANY),
            pl.BlockSpec(memory_space=pltpu.VMEM),
        ],
        out_specs=pl.BlockSpec(memory_space=pltpu.VMEM),
        scratch_shapes=[
            pltpu.VMEM(wshape, jnp.float32),
            pltpu.VMEM(wshape, jnp.float32),
            pltpu.VMEM(wshape, jnp.bfloat16),
            pltpu.VMEM(wshape, jnp.bfloat16),
            pltpu.VMEM(wshape, jnp.bfloat16),
            pltpu.VMEM(wshape, jnp.bfloat16),
            pltpu.VMEM((transitions.shape[0], half) + transitions.shape[2:], jnp.float32),
            pltpu.VMEM((transitions.shape[0], half) + transitions.shape[2:], jnp.float32),
            pltpu.VMEM((2 * transitions.shape[0], half, tile, 2 * tile), jnp.bfloat16),
            pltpu.VMEM((2 * transitions.shape[0], half, tile, 2 * tile), jnp.bfloat16),
            pltpu.SemaphoreType.DMA((3,)),
            pltpu.SemaphoreType.DMA((2, HALVES, 2)),
            pltpu.SemaphoreType.DMA((2, HALVES, 2)),
        ],
        compiler_params=pltpu.CompilerParams(
            collective_id=0, has_side_effects=True, vmem_limit_bytes=60 * 1024 * 1024),
    )(pos, transitions, tgt)
    return out.transpose(1, 2, 0, 3).reshape(rb * tile, ksets)


def solution(mesh):
    return jax.shard_map(
        per_device,
        mesh=mesh,
        in_specs=(P("act", "states", None, None, None), P(None, "states", None), P("states", None)),
        out_specs=P("states", None),
        check_vma=False,
    )
```

time: 151 us -> 167 us (1.11)
  local copies, waits for them, and re-layouts: 2.3 us -> 9.56 us
  Pallas kernels: 148 us -> 155 us
    reshape x0 -> x4, local copies, waits for them, and re-layouts: none -> 9.45 us  [the longest x2 5.35 us: per_device(): return out.transpose(1, 2, 0, 3).reshape(rb * tile, ksets)]
    pallas_call x1, Pallas kernels: 148 us -> 155 us  [per_device(): pl.pallas_call(functools.partial(sweep_kernel, n_states), out_shape=jax.S...]
    unnamed x3 -> x0, local copies, waits for them, and re-layouts: 2.19 us -> none
where the time goes in v4:
time: 167 us; the launch traced here: 166 us
  Pallas kernels  155 us (93%)
  local copies, waits for them, and re-layouts  9.56 us (6%)
    pallas_call x1, Pallas kernels, per_device(): pl.pallas_call(functools.partial(sweep_kernel, n_states), out_shape=jax.S...  155 us
    reshape x2, local copies, waits for them, and re-layouts, per_device(): return out.transpose(1, 2, 0, 3).reshape(rb * tile, ksets)  5.35 us
    reshape x2, local copies, waits for them, and re-layouts, per_device(): tgt = targets.reshape(rb, tile, HALVES, kh).transpose(2, 0, 1, 3)  4.11 us

profile of v4, /device:TPU:0, one launch (start us, length us, event | category | flops | bytes accessed | tf_op | source)
XLA Modules:
  0.0 165.6 jit_solution(18066971906712583954)
XLA Ops:
  0.0 0.7 broadcast_subtract_fusion
  0.7 0.1 copy.13
  0.8 0.6 negate_select_fusion.pos_ref
  1.4 2.5 %reshape.8 = s32[16,128,2,64]{3,2,1,0:T(2,128)S(1)} reshape(s32[2048,128]{1,0:T(8,128)} %param.5) | data formatting | bytes 2097152 | tf_op jit(solution)/shard_map/reshape | solution.py:162
  3.9 1.6 copy.23
  5.5 154.7 %shard_map.37 = f32[2,16,128,64]{3,2,1,0:T(8,128)} custom-call(s32[4,16,2]{2,1,0:T(8,128)} %negate_select_fusion.pos_ref, f32[2,16,2,128,128]{4,3,2,1,0:T(8,128)} %trans_hbm.1, s32[2,16,128,64]{3,2,1,0:T(8,128)} %bitcast.6), custom_call_target="tpu_custom_call" | custom-call | tf_op jit(solution)/shard_map/pallas_call | solution.py:165
  160.3 3.2 %copy.20 = f32[16,128,2,64]{3,2,1,0:T(2,128)S(1)} copy(f32[16,128,2,64]{3,1,0,2:T(8,128)} %bitcast.7) | data formatting | bytes 2097152 | tf_op jit(solution)/shard_map/reshape | solution.py:192
  163.5 2.1 %reshape.9 = f32[2048,128]{1,0:T(8,128)} reshape(f32[16,128,2,64]{3,2,1,0:T(2,128)S(1)} %copy.20) | data formatting | bytes 2097152 | tf_op jit(solution)/shard_map/reshape | solution.py:192

commit v5 on v4

--- a/solution.py
+++ b/solution.py
@@ -75,8 +75,8 @@
             for t in range(tv.shape[2]):
                 v = tv[al, jj, t]
                 b = v.astype(jnp.bfloat16)
-                thi[first + al, jj, :, pl.ds(t * tile, tile)] = b
-                tlo[first + al, jj, :, pl.ds(t * tile, tile)] = (
+                thi[first + al, jj, pl.ds(t * tile, tile), :] = b
+                tlo[first + al, jj, pl.ds(t * tile, tile), :] = (
                     v - b.astype(jnp.float32)).astype(jnp.bfloat16)
             return carry
 
@@ -110,13 +110,13 @@
                 a = lax.rem(2 * c + ab, 2 * acts)
                 p0 = pos_ref[a, j, 0]
                 p1 = pos_ref[a, j, 1]
-                vh = jnp.concatenate([src_hi[h, p0], src_hi[h, p1]], axis=0)
-                vl = jnp.concatenate([src_lo[h, p0], src_lo[h, p1]], axis=0)
+                vh = jnp.concatenate([src_hi[h, p0], src_hi[h, p1]], axis=1)
+                vl = jnp.concatenate([src_lo[h, p0], src_lo[h, p1]], axis=1)
                 th = thi[ab, jj]
                 tl = tlo[ab, jj]
-                q = jnp.dot(th, vh, preferred_element_type=jnp.float32)
-                q = q + jnp.dot(th, vl, preferred_element_type=jnp.float32)
-                q = q + jnp.dot(tl, vh, preferred_element_type=jnp.float32)
+                q = jnp.dot(vh, th, preferred_element_type=jnp.float32)
+                q = q + jnp.dot(vl, th, preferred_element_type=jnp.float32)
+                q = q + jnp.dot(vh, tl, preferred_element_type=jnp.float32)
                 best = q if best is None else jnp.maximum(best, q)
             val = jnp.where(tgt_ref[h, j] == 1, jnp.float32(1.0), best)
             dst_win[h, own_pos + jj] = val
@@ -159,12 +159,13 @@
     total_blocks = rb * n_states
     first = lax.axis_index("states") * rb - REACH
     pos = lax.rem(columns - first + 2 * total_blocks, total_blocks).astype(jnp.int32)
-    tgt = targets.reshape(rb, tile, HALVES, kh).transpose(2, 0, 1, 3)
+    tgt = targets.reshape(rb, tile, HALVES, kh).transpose(2, 0, 3, 1)
+    trans_t = jnp.swapaxes(transitions, -1, -2)
     half = rb // 2
-    wshape = (HALVES, rb + 2 * REACH, tile, kh)
+    wshape = (HALVES, rb + 2 * REACH, kh, tile)
     out = pl.pallas_call(
         functools.partial(sweep_kernel, n_states),
-        out_shape=jax.ShapeDtypeStruct((HALVES, rb, tile, kh), jnp.float32),
+        out_shape=jax.ShapeDtypeStruct((HALVES, rb, kh, tile), jnp.float32),
         in_specs=[
             pl.BlockSpec(memory_space=pltpu.SMEM),
             pl.BlockSpec(memory_space=pl.ANY),
@@ -180,16 +181,16 @@
             pltpu.VMEM(wshape, jnp.bfloat16),
             pltpu.VMEM((transitions.shape[0], half) + transitions.shape[2:], jnp.float32),
             pltpu.VMEM((transitions.shape[0], half) + transitions.shape[2:], jnp.float32),
-            pltpu.VMEM((2 * transitions.shape[0], half, tile, 2 * tile), jnp.bfloat16),
-            pltpu.VMEM((2 * transitions.shape[0], half, tile, 2 * tile), jnp.bfloat16),
+            pltpu.VMEM((2 * transitions.shape[0], half, 2 * tile, tile), jnp.bfloat16),
+            pltpu.VMEM((2 * transitions.shape[0], half, 2 * tile, tile), jnp.bfloat16),
             pltpu.SemaphoreType.DMA((3,)),
             pltpu.SemaphoreType.DMA((2, HALVES, 2)),
             pltpu.SemaphoreType.DMA((2, HALVES, 2)),
         ],
         compiler_params=pltpu.CompilerParams(
             collective_id=0, has_side_effects=True, vmem_limit_bytes=60 * 1024 * 1024),
-    )(pos, transitions, tgt)
-    return out.transpose(1, 2, 0, 3).reshape(rb * tile, ksets)
+    )(pos, trans_t, tgt)
+    return out.transpose(1, 3, 0, 2).reshape(rb * tile, ksets)
 
 
 def solution(mesh):

time: 167 us -> 130 us (0.78)
  Pallas kernels: 155 us -> 112 us
  local copies, waits for them, and re-layouts: 9.56 us -> 14.9 us
    pallas_call x1, Pallas kernels: 155 us -> 112 us  [per_device(): pl.pallas_call(functools.partial(sweep_kernel, n_states), out_shape=jax.S...]
    unnamed x0 -> x1, local copies, waits for them, and re-layouts: none -> 5.39 us
where the time goes in v5:
time: 130 us; the launch traced here: 128 us
  Pallas kernels  112 us (86%)
  local copies, waits for them, and re-layouts  14.9 us (11%)
  other arithmetic  1.3 us (1%)
    pallas_call x1, Pallas kernels, per_device(): pl.pallas_call(functools.partial(sweep_kernel, n_states), out_shape=jax.S...  112 us
    unnamed x1, local copies, waits for them, and re-layouts  5.39 us
    reshape x2, local copies, waits for them, and re-layouts, per_device(): return out.transpose(1, 3, 0, 2).reshape(rb * tile, ksets)  4.87 us
    reshape x2, local copies, waits for them, and re-layouts, per_device(): tgt = targets.reshape(rb, tile, HALVES, kh).transpose(2, 0, 3, 1)  4.58 us

profile of v5, /device:TPU:0, one launch (start us, length us, event | category | flops | bytes accessed | tf_op | source)
XLA Modules:
  0.0 128.0 jit_solution(10456009675661677205)
XLA Ops:
  0.0 0.7 broadcast_subtract_fusion
  0.7 0.1 copy.15
  0.8 0.6 negate_select_fusion.pos_ref
  1.4 2.5 %reshape.8 = s32[16,128,2,64]{3,2,1,0:T(2,128)S(1)} reshape(s32[2048,128]{1,0:T(8,128)} %param.5) | data formatting | bytes 2097152 | tf_op jit(solution)/shard_map/reshape | solution.py:162
  3.9 2.1 %copy.18 = s32[16,128,2,64]{1,3,0,2:T(8,128)} copy(s32[16,128,2,64]{3,2,1,0:T(2,128)S(1)} %reshape.8) | data formatting | bytes 2097152 | tf_op jit(solution)/shard_map/reshape | solution.py:162
  6.0 5.4 %copy.16 = f32[2,16,2,128,128]{3,4,2,1,0:T(8,128)} copy(f32[2,16,2,128,128]{4,3,2,1,0:T(8,128)} %param.3) | data formatting | bytes 8388608 | tf_op args[0]
  11.4 111.7 %shard_map.37 = f32[2,16,64,128]{3,2,1,0:T(8,128)} custom-call(s32[4,16,2]{2,1,0:T(8,128)} %negate_select_fusion.pos_ref, f32[2,16,2,128,128]{4,3,2,1,0:T(8,128)} %bitcast.5, s32[2,16,64,128]{3,2,1,0:T(8,128)} %bitcast.6), custom_call_target="tpu_custom_call" | custom-call | tf_op jit(solution)/shard_map/pallas_call | solution.py:166
  123.1 2.7 %copy.23 = f32[16,128,2,64]{3,2,1,0:T(2,128)S(1)} copy(f32[16,128,2,64]{1,3,0,2:T(8,128)} %bitcast.7) | data formatting | bytes 2097152 | tf_op jit(solution)/shard_map/reshape | solution.py:193
  125.9 2.1 %reshape.9 = f32[2048,128]{1,0:T(8,128)} reshape(f32[16,128,2,64]{3,2,1,0:T(2,128)S(1)} %copy.23) | data formatting | bytes 2097152 | tf_op jit(solution)/shard_map/reshape | solution.py:193

commit v6 on v5

--- a/solution.py
+++ b/solution.py
@@ -24,8 +24,8 @@
     lax.fori_loop(0, count, body, 0)
 
 
-def sweep_kernel(n_states, pos_ref, trans_hbm, tgt_ref, out_ref,
-                 win0, win1, hi0, hi1, lo0, lo1, t_own, t_oth, thi, tlo,
+def sweep_kernel(n_states, pos_ref, trans_hbm, tgt_in, out_ref,
+                 win0, win1, hi0, hi1, lo0, lo1, t_own, t_oth, thi, tlo, tgt_ref,
                  tsem, send_sem, recv_sem):
     i = lax.axis_index("states")
     c = lax.axis_index("act")
@@ -55,8 +55,18 @@
             send_sem=send_sem.at[slot, h, k], recv_sem=recv_sem.at[slot, h, k],
             device_id=dev, device_id_type=MESH)
 
-    for h in range(HALVES):
-        win0[h, pl.ds(half, 2 * half)] = tgt_ref[h].astype(jnp.float32)
+    kh = win0.shape[2]
+
+    def load_targets(b, carry):
+        tf = jnp.transpose(tgt_in[b].astype(jnp.float32))
+        for h in range(HALVES):
+            part = tf[h * kh:(h + 1) * kh]
+            tgt_ref[h, b] = part
+            win0[h, half + b] = part
+        return carry
+
+    lax.fori_loop(0, 2 * half, load_targets, 0)
+    for h in range(HALVES):
         copy_to(0, h, 1, own_pos, half, nb_halo_pos).start()
 
     own_copy = pltpu.make_async_copy(trans_hbm.at[:, pl.ds(half * c, half)], t_own, tsem.at[0])
@@ -73,7 +83,7 @@
             al = k // half
             jj = k % half
             for t in range(tv.shape[2]):
-                v = tv[al, jj, t]
+                v = jnp.transpose(tv[al, jj, t])
                 b = v.astype(jnp.bfloat16)
                 thi[first + al, jj, pl.ds(t * tile, tile), :] = b
                 tlo[first + al, jj, pl.ds(t * tile, tile), :] = (
@@ -118,7 +128,7 @@
                 q = q + jnp.dot(vl, th, preferred_element_type=jnp.float32)
                 q = q + jnp.dot(vh, tl, preferred_element_type=jnp.float32)
                 best = q if best is None else jnp.maximum(best, q)
-            val = jnp.where(tgt_ref[h, j] == 1, jnp.float32(1.0), best)
+            val = jnp.where(tgt_ref[h, j] == 1.0, jnp.float32(1.0), best)
             dst_win[h, own_pos + jj] = val
             b = val.astype(jnp.bfloat16)
             dst_hi[h, own_pos + jj] = b
@@ -147,7 +157,13 @@
         done = copy_to(0, h, 0, own_pos, half, part_pos)
         done.wait_send()
         done.wait_recv()
-        out_ref[h] = win0[h, pl.ds(half, 2 * half)]
+
+    def store_out(b, carry):
+        both = jnp.concatenate([win0[h, half + b] for h in range(HALVES)], axis=0)
+        out_ref[b] = jnp.transpose(both)
+        return carry
+
+    lax.fori_loop(0, 2 * half, store_out, 0)
 
 
 def per_device(transitions, columns, targets):
@@ -159,13 +175,12 @@
     total_blocks = rb * n_states
     first = lax.axis_index("states") * rb - REACH
     pos = lax.rem(columns - first + 2 * total_blocks, total_blocks).astype(jnp.int32)
-    tgt = targets.reshape(rb, tile, HALVES, kh).transpose(2, 0, 3, 1)
-    trans_t = jnp.swapaxes(transitions, -1, -2)
+    tgt = targets.reshape(rb, tile, ksets)
     half = rb // 2
     wshape = (HALVES, rb + 2 * REACH, kh, tile)
     out = pl.pallas_call(
         functools.partial(sweep_kernel, n_states),
-        out_shape=jax.ShapeDtypeStruct((HALVES, rb, kh, tile), jnp.float32),
+        out_shape=jax.ShapeDtypeStruct((rb, tile, ksets), jnp.float32),
         in_specs=[
             pl.BlockSpec(memory_space=pltpu.SMEM),
             pl.BlockSpec(memory_space=pl.ANY),
@@ -183,14 +198,15 @@
             pltpu.VMEM((transitions.shape[0], half) + transitions.shape[2:], jnp.float32),
             pltpu.VMEM((2 * transitions.shape[0], half, 2 * tile, tile), jnp.bfloat16),
             pltpu.VMEM((2 * transitions.shape[0], half, 2 * tile, tile), jnp.bfloat16),
+            pltpu.VMEM((HALVES, rb, kh, tile), jnp.float32),
             pltpu.SemaphoreType.DMA((3,)),
             pltpu.SemaphoreType.DMA((2, HALVES, 2)),
             pltpu.SemaphoreType.DMA((2, HALVES, 2)),
         ],
         compiler_params=pltpu.CompilerParams(
             collective_id=0, has_side_effects=True, vmem_limit_bytes=60 * 1024 * 1024),
-    )(pos, trans_t, tgt)
-    return out.transpose(1, 3, 0, 2).reshape(rb * tile, ksets)
+    )(pos, transitions, tgt)
+    return out.reshape(rb * tile, ksets)
 
 
 def solution(mesh):

time: 130 us -> 120 us (0.923)
  local copies, waits for them, and re-layouts: 14.9 us -> 2.37 us
  Pallas kernels: 112 us -> 115 us
    reshape x4 -> x0, local copies, waits for them, and re-layouts: 9.45 us -> none  [the longest x2 4.87 us: per_device(): return out.transpose(1, 3, 0, 2).reshape(rb * tile, ksets)]
    pallas_call x1, Pallas kernels: 112 us -> 115 us  [per_device(): pl.pallas_call(functools.partial(sweep_kernel, n_states), out_shape=jax.S...]
    unnamed x1, local copies, waits for them, and re-layouts: 5.39 us -> 2.26 us
where the time goes in v6:
time: 120 us; the launch traced here: 119 us
  Pallas kernels  115 us (96%)
  local copies, waits for them, and re-layouts  2.37 us (2%)
  other arithmetic  1.32 us (1%)
    pallas_call x1, Pallas kernels, per_device(): pl.pallas_call(functools.partial(sweep_kernel, n_states), out_shape=jax.S...  115 us

profile of v6, /device:TPU:0, one launch (start us, length us, event | category | flops | bytes accessed | tf_op | source)
XLA Modules:
  0.0 118.6 jit_solution(13866927594352200898)
XLA Ops:
  0.0 0.7 broadcast_subtract_fusion
  0.7 0.1 copy.7
  0.8 0.6 negate_select_fusion.pos_ref
  1.4 114.9 %shard_map.37 = f32[16,128,128]{2,1,0:T(8,128)} custom-call(s32[4,16,2]{2,1,0:T(8,128)} %negate_select_fusion.pos_ref, f32[2,16,2,128,128]{4,3,2,1,0:T(8,128)} %trans_hbm.1, s32[16,128,128]{2,1,0:T(8,128)} %bitcast.5), custom_call_target="tpu_custom_call" | custom-call | tf_op jit(solution)/shard_map/pallas_call | solution.py:181
  116.3 2.3 %copy.9 = f32[2048,128]{1,0:T(8,128)} copy(f32[2048,128]{1,0:T(8,128)} %bitcast.4) | data formatting | bytes 2097152

commit v7 on v6

--- a/solution.py
+++ b/solution.py
@@ -38,17 +38,20 @@
     nb_halo_pos = 3 * half * (1 - c)
     partner = (i, 1 - c)
     neighbour = (lax.rem(i + 2 * c - 1 + n_states, n_states), 1 - c)
+    fwd_dev = (lax.rem(i + 1 - 2 * c + n_states, n_states), c)
+    fwd_src = (lax.rem(i + 2 * c - 1 + n_states, n_states), c)
     wins = (win0, win1)
     his = (hi0, hi1)
     los = (lo0, lo1)
 
     barrier = pltpu.get_barrier_semaphore()
-    for dev in (partner, neighbour):
+    for dev in (partner, neighbour, fwd_dev, fwd_src):
         pl.semaphore_signal(barrier, inc=1, device_id=dev, device_id_type=MESH)
-    pl.semaphore_wait(barrier, 2)
-
-    def copy_to(slot, h, k, start, count, dst_start):
-        dev = partner if k == 0 else neighbour
+    pl.semaphore_wait(barrier, 4)
+
+    def copy_to(slot, h, k, start, count, dst_start, dev=None):
+        if dev is None:
+            dev = partner if k == 0 else neighbour
         return pltpu.make_async_remote_copy(
             src_ref=wins[slot].at[h, pl.ds(start, count)],
             dst_ref=wins[slot].at[h, pl.ds(dst_start, count)],
@@ -104,12 +107,22 @@
             done.wait_send()
             done.wait_recv()
             split_blocks(wins[src], his[src], los[src], h, halo_pos, half)
-        else:
+        elif h == 0:
+            got = copy_to(src, 1, 0, own_pos, half, part_pos)
+            got.wait_recv()
+            copy_to(src, 1, 1, part_pos, half, halo_pos, dev=fwd_dev).start()
+            split_blocks(wins[src], his[src], los[src], 1, part_pos, half)
             for k, start in ((0, part_pos), (1, halo_pos)):
                 done = copy_to(src, h, k, own_pos, half, start)
                 done.wait_send()
                 done.wait_recv()
                 split_blocks(wins[src], his[src], los[src], h, start, half)
+        else:
+            copy_to(src, h, 0, own_pos, half, part_pos).wait_send()
+            done = copy_to(src, h, 1, part_pos, half, halo_pos, dev=fwd_dev)
+            done.wait_send()
+            done.wait_recv()
+            split_blocks(wins[src], his[src], los[src], h, halo_pos, half)
         src_hi, src_lo = his[src], los[src]
         dst_win, dst_hi, dst_lo = wins[dst], his[dst], los[dst]
 
@@ -134,7 +147,7 @@
             dst_hi[h, own_pos + jj] = b
             dst_lo[h, own_pos + jj] = (val - b.astype(jnp.float32)).astype(jnp.bfloat16)
             copy_to(dst, h, 0, own_pos + jj, 1, own_pos + jj).start()
-            if halo:
+            if halo and h == 0:
                 copy_to(dst, h, 1, own_pos + jj, 1, nb_halo_pos + jj).start()
             return carry
 

time: 120 us -> 177 us (1.48)
  Pallas kernels: 115 us -> 171 us
    pallas_call x1, Pallas kernels: 115 us -> 171 us  [per_device(): pl.pallas_call(functools.partial(sweep_kernel, n_states), out_shape=jax.S...]
where the time goes in v7:
time: 177 us; the launch traced here: 175 us
  Pallas kernels  171 us (97%)
  local copies, waits for them, and re-layouts  2.37 us (1%)
    pallas_call x1, Pallas kernels, per_device(): pl.pallas_call(functools.partial(sweep_kernel, n_states), out_shape=jax.S...  171 us

profile of v7, /device:TPU:0, one launch (start us, length us, event | category | flops | bytes accessed | tf_op | source)
XLA Modules:
  0.0 175.1 jit_solution(463656198725990267)
XLA Ops:
  0.0 0.7 broadcast_subtract_fusion
  0.7 0.1 copy.7
  0.8 0.6 negate_select_fusion.pos_ref
  1.4 171.4 %shard_map.37 = f32[16,128,128]{2,1,0:T(8,128)} custom-call(s32[4,16,2]{2,1,0:T(8,128)} %negate_select_fusion.pos_ref, f32[2,16,2,128,128]{4,3,2,1,0:T(8,128)} %trans_hbm.1, s32[16,128,128]{2,1,0:T(8,128)} %bitcast.5), custom_call_target="tpu_custom_call" | custom-call | tf_op jit(solution)/shard_map/pallas_call | solution.py:194
  172.8 2.3 %copy.9 = f32[2048,128]{1,0:T(8,128)} copy(f32[2048,128]{1,0:T(8,128)} %bitcast.4) | data formatting | bytes 2097152

commit v8 on v7

--- a/solution.py
+++ b/solution.py
@@ -10,6 +10,7 @@
 REACH = 8
 SWEEPS = 12
 HALVES = 2
+LAG = 2
 MESH = pl.DeviceIdType.MESH
 
 
@@ -26,7 +27,7 @@
 
 def sweep_kernel(n_states, pos_ref, trans_hbm, tgt_in, out_ref,
                  win0, win1, hi0, hi1, lo0, lo1, t_own, t_oth, thi, tlo, tgt_ref,
-                 tsem, send_sem, recv_sem):
+                 tsem, send_sem, recv_sem, part_sem):
     i = lax.axis_index("states")
     c = lax.axis_index("act")
     acts = t_own.shape[0]
@@ -49,14 +50,25 @@
         pl.semaphore_signal(barrier, inc=1, device_id=dev, device_id_type=MESH)
     pl.semaphore_wait(barrier, 4)
 
-    def copy_to(slot, h, k, start, count, dst_start, dev=None):
+    def copy_to(slot, h, k, start, count, dst_start, dev=None, rsem=None):
         if dev is None:
             dev = partner if k == 0 else neighbour
+        if rsem is None:
+            rsem = recv_sem.at[slot, h, k]
         return pltpu.make_async_remote_copy(
             src_ref=wins[slot].at[h, pl.ds(start, count)],
             dst_ref=wins[slot].at[h, pl.ds(dst_start, count)],
-            send_sem=send_sem.at[slot, h, k], recv_sem=recv_sem.at[slot, h, k],
+            send_sem=send_sem.at[slot, h, k], recv_sem=rsem,
             device_id=dev, device_id_type=MESH)
+
+    def part_block(slot, jj, incoming=False):
+        if incoming:
+            return copy_to(slot, 1, 0, part_pos + jj, 1, part_pos + jj, rsem=part_sem.at[slot, jj])
+        return copy_to(slot, 1, 0, own_pos + jj, 1, own_pos + jj, rsem=part_sem.at[slot, jj])
+
+    def forward(slot, jj):
+        part_block(slot, jj, incoming=True).wait_recv()
+        copy_to(slot, 1, 1, part_pos + jj, 1, halo_pos + jj, dev=fwd_dev).start()
 
     kh = win0.shape[2]
 
@@ -108,10 +120,6 @@
             done.wait_recv()
             split_blocks(wins[src], his[src], los[src], h, halo_pos, half)
         elif h == 0:
-            got = copy_to(src, 1, 0, own_pos, half, part_pos)
-            got.wait_recv()
-            copy_to(src, 1, 1, part_pos, half, halo_pos, dev=fwd_dev).start()
-            split_blocks(wins[src], his[src], los[src], 1, part_pos, half)
             for k, start in ((0, part_pos), (1, halo_pos)):
                 done = copy_to(src, h, k, own_pos, half, start)
                 done.wait_send()
@@ -119,6 +127,7 @@
                 split_blocks(wins[src], his[src], los[src], h, start, half)
         else:
             copy_to(src, h, 0, own_pos, half, part_pos).wait_send()
+            split_blocks(wins[src], his[src], los[src], h, part_pos, half)
             done = copy_to(src, h, 1, part_pos, half, halo_pos, dev=fwd_dev)
             done.wait_send()
             done.wait_recv()
@@ -146,12 +155,27 @@
             b = val.astype(jnp.bfloat16)
             dst_hi[h, own_pos + jj] = b
             dst_lo[h, own_pos + jj] = (val - b.astype(jnp.float32)).astype(jnp.bfloat16)
-            copy_to(dst, h, 0, own_pos + jj, 1, own_pos + jj).start()
-            if halo and h == 0:
-                copy_to(dst, h, 1, own_pos + jj, 1, nb_halo_pos + jj).start()
+            if h == 0:
+                copy_to(dst, h, 0, own_pos + jj, 1, own_pos + jj).start()
+                if halo:
+                    copy_to(dst, h, 1, own_pos + jj, 1, nb_halo_pos + jj).start()
+            else:
+                part_block(dst, jj).start()
             return carry
 
-        lax.fori_loop(0, half, block, 0)
+        def block_fwd(jj, carry):
+            block(jj, carry)
+            forward(dst, jj - LAG)
+            return carry
+
+        if h == 1 and halo:
+            lax.fori_loop(0, LAG, block, 0)
+            lax.fori_loop(LAG, half, block_fwd, 0)
+        else:
+            lax.fori_loop(0, half, block, 0)
+        if h == 1 and halo:
+            for jj in range(half - LAG, half):
+                forward(dst, jj)
 
     for h in range(HALVES):
         stage(h, 0, 1, first=True)
@@ -166,10 +190,12 @@
     lax.fori_loop(0, SWEEPS // 2 - 1, pair, 0)
     for h in range(HALVES):
         stage(h, 1, 0, halo=False)
-    for h in range(HALVES):
-        done = copy_to(0, h, 0, own_pos, half, part_pos)
-        done.wait_send()
-        done.wait_recv()
+    done = copy_to(0, 0, 0, own_pos, half, part_pos)
+    done.wait_send()
+    done.wait_recv()
+    copy_to(0, 1, 0, own_pos, half, part_pos).wait_send()
+    for jj in range(half):
+        part_block(0, jj, incoming=True).wait_recv()
 
     def store_out(b, carry):
         both = jnp.concatenate([win0[h, half + b] for h in range(HALVES)], axis=0)
@@ -215,6 +241,7 @@
             pltpu.SemaphoreType.DMA((3,)),
             pltpu.SemaphoreType.DMA((2, HALVES, 2)),
             pltpu.SemaphoreType.DMA((2, HALVES, 2)),
+            pltpu.SemaphoreType.DMA((2, half)),
         ],
         compiler_params=pltpu.CompilerParams(
             collective_id=0, has_side_effects=True, vmem_limit_bytes=60 * 1024 * 1024),

time: 177 us -> 139 us (0.79)
  Pallas kernels: 171 us -> 134 us
    pallas_call x1, Pallas kernels: 171 us -> 134 us  [per_device(): pl.pallas_call(functools.partial(sweep_kernel, n_states), out_shape=jax.S...]
where the time goes in v8:
time: 139 us; the launch traced here: 137 us
  Pallas kernels  134 us (96%)
  local copies, waits for them, and re-layouts  2.37 us (2%)
    pallas_call x1, Pallas kernels, per_device(): pl.pallas_call(functools.partial(sweep_kernel, n_states), out_shape=jax.S...  134 us

profile of v8, /device:TPU:0, one launch (start us, length us, event | category | flops | bytes accessed | tf_op | source)
XLA Modules:
  0.0 137.3 jit_solution(1499222736939194794)
XLA Ops:
  0.0 0.7 broadcast_subtract_fusion
  0.7 0.1 copy.7
  0.8 0.6 negate_select_fusion.pos_ref
  1.4 133.6 %shard_map.37 = f32[16,128,128]{2,1,0:T(8,128)} custom-call(s32[4,16,2]{2,1,0:T(8,128)} %negate_select_fusion.pos_ref, f32[2,16,2,128,128]{4,3,2,1,0:T(8,128)} %trans_hbm.1, s32[16,128,128]{2,1,0:T(8,128)} %bitcast.5), custom_call_target="tpu_custom_call" | custom-call | tf_op jit(solution)/shard_map/pallas_call | solution.py:220
  135.0 2.3 %copy.9 = f32[2048,128]{1,0:T(8,128)} copy(f32[2048,128]{1,0:T(8,128)} %bitcast.4) | data formatting | bytes 2097152

commit v9 on v6

--- a/solution.py
+++ b/solution.py
@@ -65,16 +65,17 @@
             win0[h, half + b] = part
         return carry
 
-    lax.fori_loop(0, 2 * half, load_targets, 0)
-    for h in range(HALVES):
-        copy_to(0, h, 1, own_pos, half, nb_halo_pos).start()
-
     own_copy = pltpu.make_async_copy(trans_hbm.at[:, pl.ds(half * c, half)], t_own, tsem.at[0])
     own_copy.start()
     oth_copy = pltpu.make_async_remote_copy(
         src_ref=trans_hbm.at[:, pl.ds(half * (1 - c), half)], dst_ref=t_oth,
         send_sem=tsem.at[1], recv_sem=tsem.at[2], device_id=partner, device_id_type=MESH)
     oth_copy.start()
+
+    lax.fori_loop(half * c, half * c + half, load_targets, 0)
+    for h in range(HALVES):
+        copy_to(0, h, 1, own_pos, half, nb_halo_pos).start()
+    lax.fori_loop(half * (1 - c), half * (1 - c) + half, load_targets, 0)
     for h in range(HALVES):
         split_blocks(win0, hi0, lo0, h, half, 2 * half)
 

time: 120 us -> 119 us (level)
  no operation moved by 1% of the time
where the time goes in v9:
time: 119 us; the launch traced here: 118 us
  Pallas kernels  114 us (96%)
  local copies, waits for them, and re-layouts  2.37 us (2%)
  other arithmetic  1.32 us (1%)
    pallas_call x1, Pallas kernels, per_device(): pl.pallas_call(functools.partial(sweep_kernel, n_states), out_shape=jax.S...  114 us

profile of v9, /device:TPU:0, one launch (start us, length us, event | category | flops | bytes accessed | tf_op | source)
XLA Modules:
  0.0 117.8 jit_solution(16807994192611186034)
XLA Ops:
  0.0 0.7 broadcast_subtract_fusion
  0.7 0.1 copy.7
  0.8 0.6 negate_select_fusion.pos_ref
  1.4 114.1 %shard_map.37 = f32[16,128,128]{2,1,0:T(8,128)} custom-call(s32[4,16,2]{2,1,0:T(8,128)} %negate_select_fusion.pos_ref, f32[2,16,2,128,128]{4,3,2,1,0:T(8,128)} %trans_hbm.1, s32[16,128,128]{2,1,0:T(8,128)} %bitcast.5), custom_call_target="tpu_custom_call" | custom-call | tf_op jit(solution)/shard_map/pallas_call | solution.py:182
  115.5 2.3 %copy.9 = f32[2048,128]{1,0:T(8,128)} copy(f32[2048,128]{1,0:T(8,128)} %bitcast.4) | data formatting | bytes 2097152

commit v10 on v9

--- a/solution.py
+++ b/solution.py
@@ -134,9 +134,9 @@
             b = val.astype(jnp.bfloat16)
             dst_hi[h, own_pos + jj] = b
             dst_lo[h, own_pos + jj] = (val - b.astype(jnp.float32)).astype(jnp.bfloat16)
-            copy_to(dst, h, 0, own_pos + jj, 1, own_pos + jj).start()
             if halo:
                 copy_to(dst, h, 1, own_pos + jj, 1, nb_halo_pos + jj).start()
+            copy_to(dst, h, 0, own_pos + jj, 1, own_pos + jj).start()
             return carry
 
         lax.fori_loop(0, half, block, 0)

time: 119 us -> 119 us (level)
  no operation moved by 1% of the time
where the time goes in v10:
time: 119 us; the launch traced here: 118 us
  Pallas kernels  114 us (96%)
  local copies, waits for them, and re-layouts  2.37 us (2%)
  other arithmetic  1.32 us (1%)
    pallas_call x1, Pallas kernels, per_device(): pl.pallas_call(functools.partial(sweep_kernel, n_states), out_shape=jax.S...  114 us

profile of v10, /device:TPU:0, one launch (start us, length us, event | category | flops | bytes accessed | tf_op | source)
XLA Modules:
  0.0 117.8 jit_solution(15798360353149573262)
XLA Ops:
  0.0 0.7 broadcast_subtract_fusion
  0.7 0.1 copy.7
  0.8 0.6 negate_select_fusion.pos_ref
  1.4 114.1 %shard_map.37 = f32[16,128,128]{2,1,0:T(8,128)} custom-call(s32[4,16,2]{2,1,0:T(8,128)} %negate_select_fusion.pos_ref, f32[2,16,2,128,128]{4,3,2,1,0:T(8,128)} %trans_hbm.1, s32[16,128,128]{2,1,0:T(8,128)} %bitcast.5), custom_call_target="tpu_custom_call" | custom-call | tf_op jit(solution)/shard_map/pallas_call | solution.py:182
  115.5 2.3 %copy.9 = f32[2048,128]{1,0:T(8,128)} copy(f32[2048,128]{1,0:T(8,128)} %bitcast.4) | data formatting | bytes 2097152

commit v11 on v10

--- a/solution.py
+++ b/solution.py
@@ -154,17 +154,18 @@
     lax.fori_loop(0, SWEEPS // 2 - 1, pair, 0)
     for h in range(HALVES):
         stage(h, 1, 0, halo=False)
+
+    def store_out(b, carry):
+        both = jnp.concatenate([win0[h, half + b] for h in range(HALVES)], axis=0)
+        out_ref[b] = jnp.transpose(both)
+        return carry
+
+    lax.fori_loop(half * c, half * c + half, store_out, 0)
     for h in range(HALVES):
         done = copy_to(0, h, 0, own_pos, half, part_pos)
         done.wait_send()
         done.wait_recv()
-
-    def store_out(b, carry):
-        both = jnp.concatenate([win0[h, half + b] for h in range(HALVES)], axis=0)
-        out_ref[b] = jnp.transpose(both)
-        return carry
-
-    lax.fori_loop(0, 2 * half, store_out, 0)
+    lax.fori_loop(half * (1 - c), half * (1 - c) + half, store_out, 0)
 
 
 def per_device(transitions, columns, targets):

time: 119 us -> 118 us (level)
  no operation moved by 1% of the time
where the time goes in v11:
time: 118 us; the launch traced here: 117 us
  Pallas kernels  113 us (96%)
  local copies, waits for them, and re-layouts  2.37 us (2%)
  other arithmetic  1.32 us (1%)
    pallas_call x1, Pallas kernels, per_device(): pl.pallas_call(functools.partial(sweep_kernel, n_states), out_shape=jax.S...  113 us

profile of v11, /device:TPU:0, one launch (start us, length us, event | category | flops | bytes accessed | tf_op | source)
XLA Modules:
  0.0 117.0 jit_solution(17697705259456022908)
XLA Ops:
  0.0 0.7 broadcast_subtract_fusion
  0.7 0.1 copy.7
  0.8 0.6 negate_select_fusion.pos_ref
  1.4 113.3 %shard_map.37 = f32[16,128,128]{2,1,0:T(8,128)} custom-call(s32[4,16,2]{2,1,0:T(8,128)} %negate_select_fusion.pos_ref, f32[2,16,2,128,128]{4,3,2,1,0:T(8,128)} %trans_hbm.1, s32[16,128,128]{2,1,0:T(8,128)} %bitcast.5), custom_call_target="tpu_custom_call" | custom-call | tf_op jit(solution)/shard_map/pallas_call | solution.py:183
  114.7 2.3 %copy.9 = f32[2048,128]{1,0:T(8,128)} copy(f32[2048,128]{1,0:T(8,128)} %bitcast.4) | data formatting | bytes 2097152

commit v12 on v11

--- a/solution.py
+++ b/solution.py
@@ -9,7 +9,7 @@
 
 REACH = 8
 SWEEPS = 12
-HALVES = 2
+HALVES = 4
 MESH = pl.DeviceIdType.MESH
 
 

time: 118 us -> 126 us (1.068)
  Pallas kernels: 113 us -> 121 us
    pallas_call x1, Pallas kernels: 113 us -> 121 us  [per_device(): pl.pallas_call(functools.partial(sweep_kernel, n_states), out_shape=jax.S...]
where the time goes in v12:
time: 126 us; the launch traced here: 124 us
  Pallas kernels  121 us (96%)
  local copies, waits for them, and re-layouts  2.37 us (2%)
  other arithmetic  1.32 us (1%)
    pallas_call x1, Pallas kernels, per_device(): pl.pallas_call(functools.partial(sweep_kernel, n_states), out_shape=jax.S...  121 us

profile of v12, /device:TPU:0, one launch (start us, length us, event | category | flops | bytes accessed | tf_op | source)
XLA Modules:
  0.0 124.4 jit_solution(15770574384252612318)
XLA Ops:
  0.0 0.7 broadcast_subtract_fusion
  0.7 0.1 copy.7
  0.8 0.6 negate_select_fusion.pos_ref
  1.4 120.7 %shard_map.37 = f32[16,128,128]{2,1,0:T(8,128)} custom-call(s32[4,16,2]{2,1,0:T(8,128)} %negate_select_fusion.pos_ref, f32[2,16,2,128,128]{4,3,2,1,0:T(8,128)} %trans_hbm.1, s32[16,128,128]{2,1,0:T(8,128)} %bitcast.5), custom_call_target="tpu_custom_call" | custom-call | tf_op jit(solution)/shard_map/pallas_call | solution.py:183
  122.1 2.3 %copy.9 = f32[2048,128]{1,0:T(8,128)} copy(f32[2048,128]{1,0:T(8,128)} %bitcast.4) | data formatting | bytes 2097152

commit v13 on v11

--- a/solution.py
+++ b/solution.py
@@ -131,12 +131,12 @@
                 best = q if best is None else jnp.maximum(best, q)
             val = jnp.where(tgt_ref[h, j] == 1.0, jnp.float32(1.0), best)
             dst_win[h, own_pos + jj] = val
+            if halo:
+                copy_to(dst, h, 1, own_pos + jj, 1, nb_halo_pos + jj).start()
+            copy_to(dst, h, 0, own_pos + jj, 1, own_pos + jj).start()
             b = val.astype(jnp.bfloat16)
             dst_hi[h, own_pos + jj] = b
             dst_lo[h, own_pos + jj] = (val - b.astype(jnp.float32)).astype(jnp.bfloat16)
-            if halo:
-                copy_to(dst, h, 1, own_pos + jj, 1, nb_halo_pos + jj).start()
-            copy_to(dst, h, 0, own_pos + jj, 1, own_pos + jj).start()
             return carry
 
         lax.fori_loop(0, half, block, 0)

time: 118 us -> 118 us (level)
  no operation moved by 1% of the time
where the time goes in v13:
time: 118 us; the launch traced here: 117 us
  Pallas kernels  113 us (96%)
  local copies, waits for them, and re-layouts  2.37 us (2%)
  other arithmetic  1.32 us (1%)
    pallas_call x1, Pallas kernels, per_device(): pl.pallas_call(functools.partial(sweep_kernel, n_states), out_shape=jax.S...  113 us

profile of v13, /device:TPU:0, one launch (start us, length us, event | category | flops | bytes accessed | tf_op | source)
XLA Modules:
  0.0 116.9 jit_solution(2516571604606482544)
XLA Ops:
  0.0 0.7 broadcast_subtract_fusion
  0.7 0.1 copy.7
  0.8 0.6 negate_select_fusion.pos_ref
  1.4 113.2 %shard_map.37 = f32[16,128,128]{2,1,0:T(8,128)} custom-call(s32[4,16,2]{2,1,0:T(8,128)} %negate_select_fusion.pos_ref, f32[2,16,2,128,128]{4,3,2,1,0:T(8,128)} %trans_hbm.1, s32[16,128,128]{2,1,0:T(8,128)} %bitcast.5), custom_call_target="tpu_custom_call" | custom-call | tf_op jit(solution)/shard_map/pallas_call | solution.py:183
  114.7 2.3 %copy.9 = f32[2048,128]{1,0:T(8,128)} copy(f32[2048,128]{1,0:T(8,128)} %bitcast.4) | data formatting | bytes 2097152

commit v14 on v13

--- a/solution.py
+++ b/solution.py
@@ -132,7 +132,9 @@
             val = jnp.where(tgt_ref[h, j] == 1.0, jnp.float32(1.0), best)
             dst_win[h, own_pos + jj] = val
             if halo:
-                copy_to(dst, h, 1, own_pos + jj, 1, nb_halo_pos + jj).start()
+                @pl.when(jj % 2 == 1)
+                def _():
+                    copy_to(dst, h, 1, own_pos + jj - 1, 2, nb_halo_pos + jj - 1).start()
             copy_to(dst, h, 0, own_pos + jj, 1, own_pos + jj).start()
             b = val.astype(jnp.bfloat16)
             dst_hi[h, own_pos + jj] = b

time: 118 us -> 121 us (1.025)
  Pallas kernels: 113 us -> 116 us
    pallas_call x1, Pallas kernels: 113 us -> 116 us  [per_device(): pl.pallas_call(functools.partial(sweep_kernel, n_states), out_shape=jax.S...]
where the time goes in v14:
time: 121 us; the launch traced here: 120 us
  Pallas kernels  116 us (96%)
  local copies, waits for them, and re-layouts  2.37 us (2%)
  other arithmetic  1.32 us (1%)
    pallas_call x1, Pallas kernels, per_device(): pl.pallas_call(functools.partial(sweep_kernel, n_states), out_shape=jax.S...  116 us

profile of v14, /device:TPU:0, one launch (start us, length us, event | category | flops | bytes accessed | tf_op | source)
XLA Modules:
  0.0 119.8 jit_solution(2854350766639086634)
XLA Ops:
  0.0 0.7 broadcast_subtract_fusion
  0.7 0.1 copy.7
  0.8 0.6 negate_select_fusion.pos_ref
  1.4 116.1 %shard_map.37 = f32[16,128,128]{2,1,0:T(8,128)} custom-call(s32[4,16,2]{2,1,0:T(8,128)} %negate_select_fusion.pos_ref, f32[2,16,2,128,128]{4,3,2,1,0:T(8,128)} %trans_hbm.1, s32[16,128,128]{2,1,0:T(8,128)} %bitcast.5), custom_call_target="tpu_custom_call" | custom-call | tf_op jit(solution)/shard_map/pallas_call | solution.py:185
  117.6 2.3 %copy.9 = f32[2048,128]{1,0:T(8,128)} copy(f32[2048,128]{1,0:T(8,128)} %bitcast.4) | data formatting | bytes 2097152

commit v15 on v13

--- a/solution.py
+++ b/solution.py
@@ -67,10 +67,12 @@
 
     own_copy = pltpu.make_async_copy(trans_hbm.at[:, pl.ds(half * c, half)], t_own, tsem.at[0])
     own_copy.start()
-    oth_copy = pltpu.make_async_remote_copy(
-        src_ref=trans_hbm.at[:, pl.ds(half * (1 - c), half)], dst_ref=t_oth,
-        send_sem=tsem.at[1], recv_sem=tsem.at[2], device_id=partner, device_id_type=MESH)
-    oth_copy.start()
+    oth_copies = [pltpu.make_async_remote_copy(
+        src_ref=trans_hbm.at[al, pl.ds(half * (1 - c), half)], dst_ref=t_oth.at[al],
+        send_sem=tsem.at[1 + 2 * al], recv_sem=tsem.at[2 + 2 * al],
+        device_id=partner, device_id_type=MESH) for al in range(t_oth.shape[0])]
+    for cp in oth_copies:
+        cp.start()
 
     lax.fori_loop(half * c, half * c + half, load_targets, 0)
     for h in range(HALVES):
@@ -79,9 +81,9 @@
     for h in range(HALVES):
         split_blocks(win0, hi0, lo0, h, half, 2 * half)
 
-    def prep(tv, first):
+    def prep(tv, first, a0, a1):
         def body(k, carry):
-            al = k // half
+            al = a0 + k // half
             jj = k % half
             for t in range(tv.shape[2]):
                 v = jnp.transpose(tv[al, jj, t])
@@ -91,13 +93,14 @@
                     v - b.astype(jnp.float32)).astype(jnp.bfloat16)
             return carry
 
-        lax.fori_loop(0, acts * half, body, 0)
+        lax.fori_loop(0, (a1 - a0) * half, body, 0)
 
     own_copy.wait()
-    prep(t_own, 0)
-    oth_copy.wait_send()
-    oth_copy.wait_recv()
-    prep(t_oth, acts)
+    prep(t_own, 0, 0, acts)
+    for al, cp in enumerate(oth_copies):
+        cp.wait_send()
+        cp.wait_recv()
+        prep(t_oth, acts, al, al + 1)
 
     def stage(h, src, dst, first=False, halo=True):
         if first:
@@ -201,7 +204,7 @@
             pltpu.VMEM((2 * transitions.shape[0], half, 2 * tile, tile), jnp.bfloat16),
             pltpu.VMEM((2 * transitions.shape[0], half, 2 * tile, tile), jnp.bfloat16),
             pltpu.VMEM((HALVES, rb, kh, tile), jnp.float32),
-            pltpu.SemaphoreType.DMA((3,)),
+            pltpu.SemaphoreType.DMA((1 + 2 * transitions.shape[0],)),
             pltpu.SemaphoreType.DMA((2, HALVES, 2)),
             pltpu.SemaphoreType.DMA((2, HALVES, 2)),
         ],

time: 118 us -> 118 us (level)
  no operation moved by 1% of the time
where the time goes in v15:
time: 118 us; the launch traced here: 117 us
  Pallas kernels  113 us (96%)
  local copies, waits for them, and re-layouts  2.37 us (2%)
  other arithmetic  1.32 us (1%)
    pallas_call x1, Pallas kernels, per_device(): pl.pallas_call(functools.partial(sweep_kernel, n_states), out_shape=jax.S...  113 us

profile of v15, /device:TPU:0, one launch (start us, length us, event | category | flops | bytes accessed | tf_op | source)
XLA Modules:
  0.0 116.9 jit_solution(5654764089528286049)
XLA Ops:
  0.0 0.7 broadcast_subtract_fusion
  0.7 0.1 copy.7
  0.8 0.6 negate_select_fusion.pos_ref
  1.4 113.3 %shard_map.37 = f32[16,128,128]{2,1,0:T(8,128)} custom-call(s32[4,16,2]{2,1,0:T(8,128)} %negate_select_fusion.pos_ref, f32[2,16,2,128,128]{4,3,2,1,0:T(8,128)} %trans_hbm.1, s32[16,128,128]{2,1,0:T(8,128)} %bitcast.5), custom_call_target="tpu_custom_call" | custom-call | tf_op jit(solution)/shard_map/pallas_call | solution.py:186
  114.7 2.3 %copy.9 = f32[2048,128]{1,0:T(8,128)} copy(f32[2048,128]{1,0:T(8,128)} %bitcast.4) | data formatting | bytes 2097152

commit v16 on v13

--- a/solution.py
+++ b/solution.py
@@ -100,17 +100,10 @@
     prep(t_oth, acts)
 
     def stage(h, src, dst, first=False, halo=True):
-        if first:
-            done = copy_to(src, h, 1, own_pos, half, halo_pos)
-            done.wait_send()
-            done.wait_recv()
-            split_blocks(wins[src], his[src], los[src], h, halo_pos, half)
-        else:
-            for k, start in ((0, part_pos), (1, halo_pos)):
-                done = copy_to(src, h, k, own_pos, half, start)
-                done.wait_send()
-                done.wait_recv()
-                split_blocks(wins[src], his[src], los[src], h, start, half)
+        links = ((1, halo_pos),) if first else ((0, part_pos), (1, halo_pos))
+        for k, start in links:
+            copy_to(src, h, k, own_pos, half, start).wait_recv()
+            split_blocks(wins[src], his[src], los[src], h, start, half)
         src_hi, src_lo = his[src], los[src]
         dst_win, dst_hi, dst_lo = wins[dst], his[dst], los[dst]
 
@@ -140,6 +133,8 @@
             return carry
 
         lax.fori_loop(0, half, block, 0)
+        for k, start in links:
+            copy_to(src, h, k, own_pos, half, start).wait_send()
 
     for h in range(HALVES):
         stage(h, 0, 1, first=True)

time: 118 us -> 118 us (level)
  no operation moved by 1% of the time
where the time goes in v16:
time: 118 us; the launch traced here: 117 us
  Pallas kernels  113 us (96%)
  local copies, waits for them, and re-layouts  2.37 us (2%)
  other arithmetic  1.32 us (1%)
    pallas_call x1, Pallas kernels, per_device(): pl.pallas_call(functools.partial(sweep_kernel, n_states), out_shape=jax.S...  113 us

profile of v16, /device:TPU:0, one launch (start us, length us, event | category | flops | bytes accessed | tf_op | source)
XLA Modules:
  0.0 116.9 jit_solution(17902820871156630214)
XLA Ops:
  0.0 0.7 broadcast_subtract_fusion
  0.7 0.1 copy.7
  0.8 0.6 negate_select_fusion.pos_ref
  1.4 113.2 %shard_map.37 = f32[16,128,128]{2,1,0:T(8,128)} custom-call(s32[4,16,2]{2,1,0:T(8,128)} %negate_select_fusion.pos_ref, f32[2,16,2,128,128]{4,3,2,1,0:T(8,128)} %trans_hbm.1, s32[16,128,128]{2,1,0:T(8,128)} %bitcast.5), custom_call_target="tpu_custom_call" | custom-call | tf_op jit(solution)/shard_map/pallas_call | solution.py:178
  114.7 2.3 %copy.9 = f32[2048,128]{1,0:T(8,128)} copy(f32[2048,128]{1,0:T(8,128)} %bitcast.4) | data formatting | bytes 2097152

commit v17 on v16

--- a/solution.py
+++ b/solution.py
@@ -100,7 +100,7 @@
     prep(t_oth, acts)
 
     def stage(h, src, dst, first=False, halo=True):
-        links = ((1, halo_pos),) if first else ((0, part_pos), (1, halo_pos))
+        links = ((1, halo_pos),) if first else ((1, halo_pos), (0, part_pos))
         for k, start in links:
             copy_to(src, h, k, own_pos, half, start).wait_recv()
             split_blocks(wins[src], his[src], los[src], h, start, half)

time: 118 us -> 119 us (level)
  no operation moved by 1% of the time
where the time goes in v17:
time: 119 us; the launch traced here: 118 us
  Pallas kernels  114 us (96%)
  local copies, waits for them, and re-layouts  2.37 us (2%)
  other arithmetic  1.32 us (1%)
    pallas_call x1, Pallas kernels, per_device(): pl.pallas_call(functools.partial(sweep_kernel, n_states), out_shape=jax.S...  114 us

profile of v17, /device:TPU:0, one launch (start us, length us, event | category | flops | bytes accessed | tf_op | source)
XLA Modules:
  0.0 117.7 jit_solution(2643772894501770093)
XLA Ops:
  0.0 0.7 broadcast_subtract_fusion
  0.7 0.1 copy.7
  0.8 0.6 negate_select_fusion.pos_ref
  1.4 114.0 %shard_map.37 = f32[16,128,128]{2,1,0:T(8,128)} custom-call(s32[4,16,2]{2,1,0:T(8,128)} %negate_select_fusion.pos_ref, f32[2,16,2,128,128]{4,3,2,1,0:T(8,128)} %trans_hbm.1, s32[16,128,128]{2,1,0:T(8,128)} %bitcast.5), custom_call_target="tpu_custom_call" | custom-call | tf_op jit(solution)/shard_map/pallas_call | solution.py:178
  115.4 2.3 %copy.9 = f32[2048,128]{1,0:T(8,128)} copy(f32[2048,128]{1,0:T(8,128)} %bitcast.4) | data formatting | bytes 2097152
